TPU v7x, 1024 devices: a whole 4x4x32 slice. The times are simulated.
1024 devices in a mesh: dcn: 8 (over y, x_lo), ctx: 32 (over z), head: 4 (over x_hi, core).
Axes of the slice: x: 4 (x_hi: 2, x_lo: 2; x = x_hi * 2 + x_lo), y: 4, z: 32, core: 2. Of those that a mesh axis runs over, the one named last changes fastest.
Arguments:
- queries: bfloat16 [65536, 64, 128], P(('dcn', 'ctx'), 'head'), may hold values from -26 to 26
- keys: bfloat16 [65536, 8, 128], P(('dcn', 'ctx'), 'head'), may hold values from -6 to 6
- values: bfloat16 [65536, 8, 128], P(('dcn', 'ctx'), 'head'), may hold values from -6 to 6
- seg_ids: int32 [65536], P(('dcn', 'ctx')), may hold values from 0 to 255, never falling along the last dimension, each value on 1 to 768 neighbouring positions
Outputs:
- attended: bfloat16 [65536, 64, 128], P(('dcn', 'ctx'), 'head')
Inputs may be any that keep to these rules, and one draw needn't show every extreme that they name: `seg_ids`: ids never fall along the sequence; every document has 1 to 768 tokens and one has exactly 768.
All inputs are finite; a program needn't handle non-finite values.
Results may differ from a plain program's by a relative error of at most 0.0025.
Values may be sent and summed in bfloat16 or wider, within the bound.
No kernel may reach another device: no remote copies, remote signals or barrier semaphores. Data moves between devices by JAX's collectives and lax.ppermute only.
A program may use at most 32 MiB of HBM per device.

v0:
```python
import jax
import jax.numpy as jnp
from jax import lax
from jax.sharding import PartitionSpec as P

STEPS = 3


def passed_along(x, axis, by):
    count = lax.axis_size(axis)
    pairs = [(i, i + by) for i in range(count) if 0 <= i + by < count]
    return lax.ppermute(x, axis, pairs)


def local(queries, keys, values, seg_ids):
    tok_rows = queries.shape[0]
    kv_local = keys.shape[1]
    head_dim = queries.shape[2]
    group_size = queries.shape[1] // kv_local
    position = lax.axis_index(("dcn", "ctx"))
    query_pos = position * tok_rows + jnp.arange(tok_rows, dtype=jnp.int32)
    grouped = queries.reshape(tok_rows, kv_local, group_size, head_dim)
    factor = head_dim ** (-0.5)

    def attend(state, key_tile, val_tile, key_seg, key_start):
        key_pos = key_start + jnp.arange(key_tile.shape[0], dtype=jnp.int32)
        mask = (
            (seg_ids[:, None] == key_seg[None, :])
            & (key_pos[None, :] <= query_pos[:, None])
            & (key_pos[None, :] >= 0)
        )

        def work(current):
            run_max, run_sum, weighted = current
            scores = (
                jnp.einsum("qkgd,skd->kgqs", grouped, key_tile, preferred_element_type=jnp.float32)
                * factor
            )
            scores = jnp.where(mask, scores, -1e30)
            new_max = jnp.maximum(run_max, jnp.max(scores, axis=-1))
            weights = jnp.where(mask, jnp.exp(scores - new_max[..., None]), 0.0)
            rescale = jnp.exp(run_max - new_max)
            new_sum = run_sum * rescale + jnp.sum(weights, axis=-1)
            update = jnp.einsum(
                "kgqs,skd->kgqd",
                weights.astype(jnp.bfloat16),
                val_tile,
                preferred_element_type=jnp.float32,
            )
            return (new_max, new_sum, weighted * rescale[..., None] + update)

        return lax.cond(jnp.any(mask), work, lambda current: current, state)

    state = (
        jnp.full((kv_local, group_size, tok_rows), -1e30, jnp.float32),
        jnp.zeros((kv_local, group_size, tok_rows), jnp.float32),
        jnp.zeros((kv_local, group_size, tok_rows, head_dim), jnp.float32),
    )
    state = attend(state, keys, values, seg_ids, position * tok_rows)

    def advance(distance, carry):
        current, carried = carry
        carried = passed_along((carried[0], carried[1], carried[2]), ("dcn", "ctx"), 1)
        current = attend(
            current, carried[0], carried[1], carried[2], (position - distance) * tok_rows
        )
        return (current, carried)

    state, _ = lax.fori_loop(1, STEPS + 1, advance, (state, (keys, values, seg_ids)))
    run_max, run_sum, weighted = state
    result = weighted / run_sum[..., None]
    return (
        result.transpose(2, 0, 1, 3)
        .reshape(tok_rows, kv_local * group_size, head_dim)
        .astype(jnp.bfloat16)
    )


def solution(mesh):
    placed = (
        P(("dcn", "ctx"), "head", None),
        P(("dcn", "ctx"), "head", None),
        P(("dcn", "ctx"), "head", None),
        P(("dcn", "ctx")),
    )
    return jax.shard_map(
        local,
        mesh=mesh,
        in_specs=placed,
        out_specs=P(("dcn", "ctx"), "head", None),
        check_vma=False,
    )
```

profile of v0, /device:TPU:24, one launch (start us, length us, event | category | flops | bytes accessed | tf_op | source)
XLA Modules:
  0.0 95.3 jit_solution(5534931546742795206)
XLA Ops:
  0.0 1.6 %and_and_fusion.1 = (pred[256,256]{0,1:T(8,128)(4,1)S(1)}, pred[]{:T(512)}) fusion(s32[256]{0:T(256)S(1)} %iota_add_fusion.2, s32[256]{0:T(256)} %param.13, pred[256]{0:T(512)(128)(4,1)S(1)} %broadcast_compare_fusion.1), kind=kLoop, calls=%fused_computation.49 | loop fusion | flops 327679 | bytes 67841 | tf_op jit(solution)/shard_map/and | solution.py:28
  3.7 7.3 %conditional.2 = (f32[2,8,256]{2,1,0:T(8,128)}, f32[2,8,256]{2,1,0:T(8,128)S(1)}, f32[2,8,256,128]{3,2,1,0:T(8,128)S(1)}) conditional(s32[]{:T(128)} %convert_element_type.25, () %tuple.34, (pred[256,256]{0,1:T(8,128)(4,1)S(1)}, bf16[256,2,128]{2,1,0:T(2,128)(2,1)}, bf16[256,2,8,128]{3,0,2,1:T(8,128)(2,1)S(1)}, bf16[256,2,128]{2,1,0:T(2,128)(2,1)}) %tuple.73), branch_computations={%region_1.0_spmd, %region_2.5_spmd} | conditional | flops 551043072 | bytes 16891956 | solution.py:52
  3.8 1.7 %fusion.2 = (f32[2,8,256]{2,1,0:T(8,128)S(1)}, f32[2,256,256,8]{2,1,3,0:T(8,128)S(1)}) fusion(pred[256,256]{0,1:T(8,128)(4,1)S(1)} %get-tuple-element.210, bf16[256,2,8,128]{3,0,2,1:T(8,128)(2,1)S(1)} %get-tuple-element.212, bf16[256,2,128,1]{2,1,0,3:T(2,128)(2,1)} %bitcast.50), kind=kOutput, calls=%fused_computation.3 | convolution fusion | flops 271577088 | bytes 5455872 | tf_op jit(solution)/shard_map/cond/branch_1_fun/qkgd,skd->kgqs/dot_general | solution.py:36
  6.1 1.7 %fusion.4 = f32[2,8,256]{2,1,0:T(8,128)S(1)} fusion(f32[2,256,256,8]{2,1,3,0:T(8,128)S(1)} %get-tuple-element.318, f32[2,8,256]{2,1,0:T(8,128)} %get-tuple-element.409, pred[256,256]{0,1:T(8,128)(4,1)S(1)} %get-tuple-element.210), kind=kLoop, calls=%fused_computation.5 | loop fusion | flops 5238784 | bytes 4292608 | tf_op jit(solution)/shard_map/cond/branch_1_fun/reduce_sum | solution.py:43
  8.6 2.4 %fusion.12 = f32[2,8,256,128]{3,2,1,0:T(8,128)S(1)} fusion(f32[2,256,256,8]{2,1,3,0:T(8,128)S(1)} %get-tuple-element.318, f32[2,8,256]{2,1,0:T(8,128)} %get-tuple-element.409, pred[256,256]{0,1:T(8,128)(4,1)S(1)} %get-tuple-element.210, f32[2,8,256]{2,1,0:T(8,128)S(1)} %get-tuple-element.311, bf16[256,2,128,1]{2,1,0,3:T(2,128)(2,1)S(1)} %bitcast.51), kind=kOutput, calls=%fused_computation.12 | convolution fusion | flops 274202624 | bytes 6520832 | tf_op jit(solution)/shard_map/cond/branch_1_fun/kgqs,skd->kgqd/dot_general | solution.py:44
  11.0 1.6 %copy.10 = bf16[256,2,128]{2,0,1:T(8,128)(2,1)} copy(bf16[256,2,128]{2,1,0:T(2,128)(2,1)} %param.11) | data formatting | bytes 262144
  12.6 1.6 %copy.11 = bf16[256,2,128]{2,0,1:T(8,128)(2,1)} copy(bf16[256,2,128]{2,1,0:T(2,128)(2,1)} %param.12) | data formatting | bytes 262144
  14.2 78.8 %while.24 = (s32[]{:T(128)}, f32[2,8,256]{2,1,0:T(8,128)}, f32[2,8,256]{2,1,0:T(8,128)S(1)}, f32[2,8,256,128]{3,2,1,0:T(8,128)S(1)}, bf16[256,2,128]{2,0,1:T(8,1...) while((s32[]{:T(128)}, f32[2,8,256]{2,1,0:T(8,128)}, ...), condition=%wide.region_11.12_spmd.clone, body=%wide.region_5.11_spmd.clone.sunk | while | flops 551887872 | bytes 20198288 | solution.py:69
  14.2 3.8 %collective-permute-start = (s32[256]{0:T(256)S(1)}, s32[256]{0:T(256)S(1)}, u32[]{:S(2)}, u32[]{:S(2)}) collective-permute-start(s32[256]{0:T(256)S(1)} %get-tuple-element.431), channel_id=1, source_target_pairs={{0,4},{4,8},{8,12},{12,16},{16,20},{20,24},{24,28},{28,32},{32,36}... | collective-permute-start | bytes 3080 | tf_op jit(solution)/shard_map/while/body/eval_jaxpr/ppermute | solution.py:12
  18.0 3.8 %collective-permute-start.1 = (bf16[256,2,128]{2,0,1:T(8,128)(2,1)}, bf16[256,2,128]{2,0,1:T(8,128)(2,1)S(1)}, u32[]{:S(2)}, u32[]{:S(2)}) collective-permute-start(bf16[256,2,128]{2,0,1:T(8,128)(2,1)} %get-tuple-element.429), channel_id=1, source_target_pairs={{0,4},{4,8},{8,12},{12,16},{16,20},{20,24},{24,28},{28,32},{32,36}... | collective-permute-start | bytes 393224 | tf_op jit(solution)/shard_map/while/body/eval_jaxpr/ppermute | solution.py:12
  21.8 3.8 %collective-permute-start.2 = (bf16[256,2,128]{2,0,1:T(8,128)(2,1)}, bf16[256,2,128]{2,0,1:T(8,128)(2,1)S(1)}, u32[]{:S(2)}, u32[]{:S(2)}) collective-permute-start(bf16[256,2,128]{2,0,1:T(8,128)(2,1)} %get-tuple-element.430), channel_id=1, source_target_pairs={{0,4},{4,8},{8,12},{12,16},{16,20},{20,24},{24,28},{28,32},{32,36}... | collective-permute-start | bytes 393224 | tf_op jit(solution)/shard_map/while/body/eval_jaxpr/ppermute | solution.py:12
  25.7 9.8 %collective-permute-done = s32[256]{0:T(256)S(1)} collective-permute-done((s32[256]{0:T(256)S(1)}, s32[256]{0:T(256)S(1)}, u32[]{:S(2)}, u32[]{:S(2)}) %collective-permute-start) | collective-permute-done | bytes 1056 | tf_op jit(solution)/shard_map/while/body/eval_jaxpr/ppermute | solution.py:12
  37.0 3.5 %collective-permute-done.1 = bf16[256,2,128]{2,0,1:T(8,128)(2,1)S(1)} collective-permute-done((bf16[256,2,128]{2,0,1:T(8,128)(2,1)}, bf16[256,2,128]{2,0,1:T(8,128)(2,1)S(1)}, u32[]{:S(2)}, u32[]{:S(2)}) %collective-permute-start.1) | collective-permute-done | bytes 131104 | tf_op jit(solution)/shard_map/while/body/eval_jaxpr/ppermute | solution.py:12
  40.4 2.0 %collective-permute-done.2 = bf16[256,2,128]{2,0,1:T(8,128)(2,1)S(1)} collective-permute-done((bf16[256,2,128]{2,0,1:T(8,128)(2,1)}, bf16[256,2,128]{2,0,1:T(8,128)(2,1)S(1)}, u32[]{:S(2)}, u32[]{:S(2)}) %collective-permute-start.2) | collective-permute-done | bytes 131104 | tf_op jit(solution)/shard_map/while/body/eval_jaxpr/ppermute | solution.py:12
  42.4 5.7 %conditional.5 = ((f32[2,8,256]{2,1,0:T(8,128)}, f32[2,8,256]{2,1,0:T(8,128)S(1)}, f32[2,8,256,128]{3,2,1,0:T(8,128)S(1)})) conditional(s32[]{:T(128)} %convert_element_type.42, (f32[2,8,256]{2,1,0:T(8,128)}, f32[2,8,256]{2,1,0:T(8,128)S(1)}, f32[2,8,256,128]{3,2,1,0:T(8,128)S(1)}) %tuple.62, (pred[256,256]{0,1:T(8,128)(4,1)S(1)}, ...), branch_computations={%region_7.7_spmd, %region_8.10_spmd} | conditional | flops 551559168 | bytes 18546720 | solution.py:52
  46.2 1.9 %multiply_add_fusion = f32[2,8,256,128]{3,2,1,0:T(8,128)S(1)} fusion(f32[2,8,256,128]{3,2,1,0:T(8,128)S(1)} %get-tuple-element.219, f32[2,256,256,8]{2,1,3,0:T(8,128)S(1)} %get-tuple-element.320, f32[2,8,256]{2,1,0:T(8,128)S(1)} %max.2, pred[256,256]{0,1:T(8,128)(4,1)S(1)} %get-tuple-element.215, f32[2,8,256]{2,1,0:T(8,128)S(1)} %get-tuple-element.314, ...), kind=kOutput, calls=%fused_computation.28 | convolution fusion | flops 274726912 | bytes 8617984 | tf_op jit(solution)/shard_map/while/body/eval_jaxpr/cond/branch_1_fun/kgqs,skd->kgqd/dot_general | solution.py:44
  49.4 1.9 %collective-permute-start = (s32[256]{0:T(256)S(1)}, s32[256]{0:T(256)S(1)}, u32[]{:S(2)}, u32[]{:S(2)}) collective-permute-start(s32[256]{0:T(256)S(1)} %get-tuple-element.431), channel_id=1, source_target_pairs={{0,4},{4,8},{8,12},{12,16},{16,20},{20,24},{24,28},{28,32},{32,36}... | collective-permute-start | bytes 3080 | tf_op jit(solution)/shard_map/while/body/eval_jaxpr/ppermute | solution.py:12
  51.3 1.9 %collective-permute-start.1 = (bf16[256,2,128]{2,0,1:T(8,128)(2,1)}, bf16[256,2,128]{2,0,1:T(8,128)(2,1)S(1)}, u32[]{:S(2)}, u32[]{:S(2)}) collective-permute-start(bf16[256,2,128]{2,0,1:T(8,128)(2,1)} %get-tuple-element.429), channel_id=1, source_target_pairs={{0,4},{4,8},{8,12},{12,16},{16,20},{20,24},{24,28},{28,32},{32,36}... | collective-permute-start | bytes 393224 | tf_op jit(solution)/shard_map/while/body/eval_jaxpr/ppermute | solution.py:12
  53.2 1.9 %collective-permute-start.2 = (bf16[256,2,128]{2,0,1:T(8,128)(2,1)}, bf16[256,2,128]{2,0,1:T(8,128)(2,1)S(1)}, u32[]{:S(2)}, u32[]{:S(2)}) collective-permute-start(bf16[256,2,128]{2,0,1:T(8,128)(2,1)} %get-tuple-element.430), channel_id=1, source_target_pairs={{0,4},{4,8},{8,12},{12,16},{16,20},{20,24},{24,28},{28,32},{32,36}... | collective-permute-start | bytes 393224 | tf_op jit(solution)/shard_map/while/body/eval_jaxpr/ppermute | solution.py:12
  55.2 2.6 %collective-permute-done = s32[256]{0:T(256)S(1)} collective-permute-done((s32[256]{0:T(256)S(1)}, s32[256]{0:T(256)S(1)}, u32[]{:S(2)}, u32[]{:S(2)}) %collective-permute-start) | collective-permute-done | bytes 1056 | tf_op jit(solution)/shard_map/while/body/eval_jaxpr/ppermute | solution.py:12
  59.3 3.2 %collective-permute-done.1 = bf16[256,2,128]{2,0,1:T(8,128)(2,1)S(1)} collective-permute-done((bf16[256,2,128]{2,0,1:T(8,128)(2,1)}, bf16[256,2,128]{2,0,1:T(8,128)(2,1)S(1)}, u32[]{:S(2)}, u32[]{:S(2)}) %collective-permute-start.1) | collective-permute-done | bytes 131104 | tf_op jit(solution)/shard_map/while/body/eval_jaxpr/ppermute | solution.py:12
  62.6 1.6 %collective-permute-done.2 = bf16[256,2,128]{2,0,1:T(8,128)(2,1)S(1)} collective-permute-done((bf16[256,2,128]{2,0,1:T(8,128)(2,1)}, bf16[256,2,128]{2,0,1:T(8,128)(2,1)S(1)}, u32[]{:S(2)}, u32[]{:S(2)}) %collective-permute-start.2) | collective-permute-done | bytes 131104 | tf_op jit(solution)/shard_map/while/body/eval_jaxpr/ppermute | solution.py:12
  64.2 5.7 %conditional.5 = ((f32[2,8,256]{2,1,0:T(8,128)}, f32[2,8,256]{2,1,0:T(8,128)S(1)}, f32[2,8,256,128]{3,2,1,0:T(8,128)S(1)})) conditional(s32[]{:T(128)} %convert_element_type.42, (f32[2,8,256]{2,1,0:T(8,128)}, f32[2,8,256]{2,1,0:T(8,128)S(1)}, f32[2,8,256,128]{3,2,1,0:T(8,128)S(1)}) %tuple.62, (pred[256,256]{0,1:T(8,128)(4,1)S(1)}, ...), branch_computations={%region_7.7_spmd, %region_8.10_spmd} | conditional | flops 551559168 | bytes 18546720 | solution.py:52
  68.1 1.9 %multiply_add_fusion = f32[2,8,256,128]{3,2,1,0:T(8,128)S(1)} fusion(f32[2,8,256,128]{3,2,1,0:T(8,128)S(1)} %get-tuple-element.219, f32[2,256,256,8]{2,1,3,0:T(8,128)S(1)} %get-tuple-element.320, f32[2,8,256]{2,1,0:T(8,128)S(1)} %max.2, pred[256,256]{0,1:T(8,128)(4,1)S(1)} %get-tuple-element.215, f32[2,8,256]{2,1,0:T(8,128)S(1)} %get-tuple-element.314, ...), kind=kOutput, calls=%fused_computation.28 | convolution fusion | flops 274726912 | bytes 8617984 | tf_op jit(solution)/shard_map/while/body/eval_jaxpr/cond/branch_1_fun/kgqs,skd->kgqd/dot_general | solution.py:44
  71.2 1.9 %collective-permute-start = (s32[256]{0:T(256)S(1)}, s32[256]{0:T(256)S(1)}, u32[]{:S(2)}, u32[]{:S(2)}) collective-permute-start(s32[256]{0:T(256)S(1)} %get-tuple-element.431), channel_id=1, source_target_pairs={{0,4},{4,8},{8,12},{12,16},{16,20},{20,24},{24,28},{28,32},{32,36}... | collective-permute-start | bytes 3080 | tf_op jit(solution)/shard_map/while/body/eval_jaxpr/ppermute | solution.py:12
  73.2 1.9 %collective-permute-start.1 = (bf16[256,2,128]{2,0,1:T(8,128)(2,1)}, bf16[256,2,128]{2,0,1:T(8,128)(2,1)S(1)}, u32[]{:S(2)}, u32[]{:S(2)}) collective-permute-start(bf16[256,2,128]{2,0,1:T(8,128)(2,1)} %get-tuple-element.429), channel_id=1, source_target_pairs={{0,4},{4,8},{8,12},{12,16},{16,20},{20,24},{24,28},{28,32},{32,36}... | collective-permute-start | bytes 393224 | tf_op jit(solution)/shard_map/while/body/eval_jaxpr/ppermute | solution.py:12
  75.1 1.9 %collective-permute-start.2 = (bf16[256,2,128]{2,0,1:T(8,128)(2,1)}, bf16[256,2,128]{2,0,1:T(8,128)(2,1)S(1)}, u32[]{:S(2)}, u32[]{:S(2)}) collective-permute-start(bf16[256,2,128]{2,0,1:T(8,128)(2,1)} %get-tuple-element.430), channel_id=1, source_target_pairs={{0,4},{4,8},{8,12},{12,16},{16,20},{20,24},{24,28},{28,32},{32,36}... | collective-permute-start | bytes 393224 | tf_op jit(solution)/shard_map/while/body/eval_jaxpr/ppermute | solution.py:12
  77.1 2.6 %collective-permute-done = s32[256]{0:T(256)S(1)} collective-permute-done((s32[256]{0:T(256)S(1)}, s32[256]{0:T(256)S(1)}, u32[]{:S(2)}, u32[]{:S(2)}) %collective-permute-start) | collective-permute-done | bytes 1056 | tf_op jit(solution)/shard_map/while/body/eval_jaxpr/ppermute | solution.py:12
  81.2 3.3 %collective-permute-done.1 = bf16[256,2,128]{2,0,1:T(8,128)(2,1)S(1)} collective-permute-done((bf16[256,2,128]{2,0,1:T(8,128)(2,1)}, bf16[256,2,128]{2,0,1:T(8,128)(2,1)S(1)}, u32[]{:S(2)}, u32[]{:S(2)}) %collective-permute-start.1) | collective-permute-done | bytes 131104 | tf_op jit(solution)/shard_map/while/body/eval_jaxpr/ppermute | solution.py:12
  85.9 5.7 %conditional.5 = ((f32[2,8,256]{2,1,0:T(8,128)}, f32[2,8,256]{2,1,0:T(8,128)S(1)}, f32[2,8,256,128]{3,2,1,0:T(8,128)S(1)})) conditional(s32[]{:T(128)} %convert_element_type.42, (f32[2,8,256]{2,1,0:T(8,128)}, f32[2,8,256]{2,1,0:T(8,128)S(1)}, f32[2,8,256,128]{3,2,1,0:T(8,128)S(1)}) %tuple.62, (pred[256,256]{0,1:T(8,128)(4,1)S(1)}, ...), branch_computations={%region_7.7_spmd, %region_8.10_spmd} | conditional | flops 551559168 | bytes 18546720 | solution.py:52
  89.8 1.9 %multiply_add_fusion = f32[2,8,256,128]{3,2,1,0:T(8,128)S(1)} fusion(f32[2,8,256,128]{3,2,1,0:T(8,128)S(1)} %get-tuple-element.219, f32[2,256,256,8]{2,1,3,0:T(8,128)S(1)} %get-tuple-element.320, f32[2,8,256]{2,1,0:T(8,128)S(1)} %max.2, pred[256,256]{0,1:T(8,128)(4,1)S(1)} %get-tuple-element.215, f32[2,8,256]{2,1,0:T(8,128)S(1)} %get-tuple-element.314, ...), kind=kOutput, calls=%fused_computation.28 | convolution fusion | flops 274726912 | bytes 8617984 | tf_op jit(solution)/shard_map/while/body/eval_jaxpr/cond/branch_1_fun/kgqs,skd->kgqd/dot_general | solution.py:44
  93.7 1.6 %copy.30 = bf16[256,2,8,128]{3,2,1,0:T(8,128)(2,1)} copy(bf16[256,2,8,128]{3,0,2,1:T(8,128)(2,1)S(1)} %fusion.40) | data formatting | bytes 2097152 | tf_op jit(solution)/shard_map/convert_element_type | solution.py:75
  (48 shorter events, 22.9 us)
Async XLA Ops:
  3.7 10.4 %copy-start.1 = (s32[256]{0:T(256)S(1)}, s32[256]{0:T(256)}, u32[]{:S(2)}) copy-start(s32[256]{0:T(256)} %param.13) | copy-start | bytes 3076
  3.8 4.8 %copy-start = (bf16[256,2,128]{2,1,0:T(2,128)(2,1)S(1)}, bf16[256,2,128]{2,1,0:T(2,128)(2,1)}, u32[]{:S(2)}) copy-start(bf16[256,2,128]{2,1,0:T(2,128)(2,1)} %get-tuple-element.277) | copy-start | bytes 393220 | tf_op jit(solution)/shard_map/cond
  14.2 21.3 %collective-permute-start = (s32[256]{0:T(256)S(1)}, s32[256]{0:T(256)S(1)}, u32[]{:S(2)}, u32[]{:S(2)}) collective-permute-start(s32[256]{0:T(256)S(1)} %get-tuple-element.431), channel_id=1, source_target_pairs={{0,4},{4,8},{8,12},{12,16},{16,20},{20,24},{24,28},{28,32},{32,36}... | collective-permute-start | bytes 3080 | tf_op jit(solution)/shard_map/while/body/eval_jaxpr/ppermute | solution.py:12
  18.0 22.4 %collective-permute-start.1 = (bf16[256,2,128]{2,0,1:T(8,128)(2,1)}, bf16[256,2,128]{2,0,1:T(8,128)(2,1)S(1)}, u32[]{:S(2)}, u32[]{:S(2)}) collective-permute-start(bf16[256,2,128]{2,0,1:T(8,128)(2,1)} %get-tuple-element.429), channel_id=1, source_target_pairs={{0,4},{4,8},{8,12},{12,16},{16,20},{20,24},{24,28},{28,32},{32,36}... | collective-permute-start | bytes 393224 | tf_op jit(solution)/shard_map/while/body/eval_jaxpr/ppermute | solution.py:12
  21.8 20.6 %collective-permute-start.2 = (bf16[256,2,128]{2,0,1:T(8,128)(2,1)}, bf16[256,2,128]{2,0,1:T(8,128)(2,1)S(1)}, u32[]{:S(2)}, u32[]{:S(2)}) collective-permute-start(bf16[256,2,128]{2,0,1:T(8,128)(2,1)} %get-tuple-element.430), channel_id=1, source_target_pairs={{0,4},{4,8},{8,12},{12,16},{16,20},{20,24},{24,28},{28,32},{32,36}... | collective-permute-start | bytes 393224 | tf_op jit(solution)/shard_map/while/body/eval_jaxpr/ppermute | solution.py:12
  49.4 8.5 %collective-permute-start = (s32[256]{0:T(256)S(1)}, s32[256]{0:T(256)S(1)}, u32[]{:S(2)}, u32[]{:S(2)}) collective-permute-start(s32[256]{0:T(256)S(1)} %get-tuple-element.431), channel_id=1, source_target_pairs={{0,4},{4,8},{8,12},{12,16},{16,20},{20,24},{24,28},{28,32},{32,36}... | collective-permute-start | bytes 3080 | tf_op jit(solution)/shard_map/while/body/eval_jaxpr/ppermute | solution.py:12
  51.3 11.3 %collective-permute-start.1 = (bf16[256,2,128]{2,0,1:T(8,128)(2,1)}, bf16[256,2,128]{2,0,1:T(8,128)(2,1)S(1)}, u32[]{:S(2)}, u32[]{:S(2)}) collective-permute-start(bf16[256,2,128]{2,0,1:T(8,128)(2,1)} %get-tuple-element.429), channel_id=1, source_target_pairs={{0,4},{4,8},{8,12},{12,16},{16,20},{20,24},{24,28},{28,32},{32,36}... | collective-permute-start | bytes 393224 | tf_op jit(solution)/shard_map/while/body/eval_jaxpr/ppermute | solution.py:12
  53.2 11.0 %collective-permute-start.2 = (bf16[256,2,128]{2,0,1:T(8,128)(2,1)}, bf16[256,2,128]{2,0,1:T(8,128)(2,1)S(1)}, u32[]{:S(2)}, u32[]{:S(2)}) collective-permute-start(bf16[256,2,128]{2,0,1:T(8,128)(2,1)} %get-tuple-element.430), channel_id=1, source_target_pairs={{0,4},{4,8},{8,12},{12,16},{16,20},{20,24},{24,28},{28,32},{32,36}... | collective-permute-start | bytes 393224 | tf_op jit(solution)/shard_map/while/body/eval_jaxpr/ppermute | solution.py:12
  71.2 8.5 %collective-permute-start = (s32[256]{0:T(256)S(1)}, s32[256]{0:T(256)S(1)}, u32[]{:S(2)}, u32[]{:S(2)}) collective-permute-start(s32[256]{0:T(256)S(1)} %get-tuple-element.431), channel_id=1, source_target_pairs={{0,4},{4,8},{8,12},{12,16},{16,20},{20,24},{24,28},{28,32},{32,36}... | collective-permute-start | bytes 3080 | tf_op jit(solution)/shard_map/while/body/eval_jaxpr/ppermute | solution.py:12
  73.2 11.4 %collective-permute-start.1 = (bf16[256,2,128]{2,0,1:T(8,128)(2,1)}, bf16[256,2,128]{2,0,1:T(8,128)(2,1)S(1)}, u32[]{:S(2)}, u32[]{:S(2)}) collective-permute-start(bf16[256,2,128]{2,0,1:T(8,128)(2,1)} %get-tuple-element.429), channel_id=1, source_target_pairs={{0,4},{4,8},{8,12},{12,16},{16,20},{20,24},{24,28},{28,32},{32,36}... | collective-permute-start | bytes 393224 | tf_op jit(solution)/shard_map/while/body/eval_jaxpr/ppermute | solution.py:12
  75.1 10.8 %collective-permute-start.2 = (bf16[256,2,128]{2,0,1:T(8,128)(2,1)}, bf16[256,2,128]{2,0,1:T(8,128)(2,1)S(1)}, u32[]{:S(2)}, u32[]{:S(2)}) collective-permute-start(bf16[256,2,128]{2,0,1:T(8,128)(2,1)} %get-tuple-element.430), channel_id=1, source_target_pairs={{0,4},{4,8},{8,12},{12,16},{16,20},{20,24},{24,28},{28,32},{32,36}... | collective-permute-start | bytes 393224 | tf_op jit(solution)/shard_map/while/body/eval_jaxpr/ppermute | solution.py:12
where the time goes:
time: 96.6 us; the launch traced here: 95.3 us
  waiting for transfers between devices  30.1 us (31%)
  starting transfers between devices  23 us (24%)
  other arithmetic  15.3 us (16%)
  matrix products  12.1 us (13%)
  local copies, waits for them, and re-layouts  12 us (12%)
  loops' own time  2.25 us (2%)
    ppermute x9, waiting for transfers between devices, passed_along(): return lax.ppermute(x, axis, pairs)  30.1 us
    ppermute x9, starting transfers between devices, passed_along(): return lax.ppermute(x, axis, pairs)  23 us
    dot_general x4, matrix products, work(): jnp.einsum('kgqs,skd->kgqd', weights.astype(jnp.bfloat16), val_tile, pref...  8.04 us
    reduce_sum x4, other arithmetic, work(): new_sum = run_sum * rescale + jnp.sum(weights, axis=-1)  4.79 us
    unnamed x6, local copies, waits for them, and re-layouts  4.64 us
    dot_general x4, matrix products, work(): jnp.einsum('qkgd,skd->kgqs', grouped, key_tile, preferred_element_type=jn...  4.01 us
    while x9, local copies, waits for them, and re-layouts  3.89 us
    add x4, other arithmetic, work(): new_sum = run_sum * rescale + jnp.sum(weights, axis=-1)  2.93 us
  transfers between devices with their start and end apart: 9, of which 9 were waited for; matrix products, arithmetic and copies ran while one was open for 3% of the time, Pallas kernels for 0%

commit v1 on v0

v1 whole, which is shorter than its diff:
```python
import jax
import jax.numpy as jnp
from jax import lax
from jax.experimental import pallas as pl
from jax.experimental.pallas import tpu as pltpu
from jax.sharding import PartitionSpec as P


AXES = ("dcn", "ctx")
LOG2E = 1.4426950408889634
NEG = -1e30
CHUNK = 32
LIMIT = 24 * 1024 * 1024

VMEM = pl.BlockSpec(memory_space=pltpu.VMEM)


def passed_along(x, by):
    count = lax.axis_size(AXES)
    pairs = [(i, i + by) for i in range(count) if 0 <= i + by < count]
    return lax.ppermute(x, AXES, pairs)


def pack_keys(k_ref, seg_ref, out_ref):
    tok, kv, _ = k_ref.shape
    keys = k_ref[...].astype(jnp.float32)
    for g in range(kv):
        out_ref[g * tok : (g + 1) * tok, :] = keys[:, g, :].astype(jnp.bfloat16)
    rows = seg_ref.shape[0]
    marks = (seg_ref[...] + 1).astype(jnp.float32)
    pad = jnp.zeros((8 - rows, 128), jnp.float32)
    out_ref[kv * tok :, :] = jnp.concatenate([marks, pad], axis=0).astype(jnp.bfloat16)


def pack_values(v_ref, out_ref):
    tok, kv, _ = v_ref.shape
    vals = v_ref[...].astype(jnp.float32)
    for g in range(kv):
        out_ref[g * tok : (g + 1) * tok, :] = vals[:, g, :].astype(jnp.bfloat16)


def dot_t(a, b):
    return lax.dot_general(a, b, (((1,), (1,)), ((), ())), preferred_element_type=jnp.float32)


def with_ones(vals):
    return jnp.concatenate([vals, jnp.ones(vals.shape, vals.dtype)], axis=1)


def queries_of(q_ref, t0, g, group):
    q = q_ref[pl.ds(t0, CHUNK), :, :].astype(jnp.float32)
    hd = q.shape[-1]
    return q[:, g * group : (g + 1) * group, :].reshape(CHUNK * group, hd).astype(jnp.bfloat16)


def key_marks(k_ref, tok):
    rows = tok // 128
    base = k_ref.shape[0] - 8
    tail = k_ref[base : base + 8, :].astype(jnp.float32)
    return jnp.concatenate([tail[r : r + 1, :] for r in range(rows)], axis=1)


def own_tile(q_ref, k_ref, v_ref, acc_ref, top_ref, bias_ref):
    tok, heads, hd = q_ref.shape
    kv = acc_ref.shape[0]
    group = heads // kv
    scale = hd**-0.5 * LOG2E
    key_seg = key_marks(k_ref, tok)
    for r in range(tok // 128):
        marks = jnp.broadcast_to(key_seg[:, r * 128 : (r + 1) * 128], (128, 128)).T
        row = lax.broadcasted_iota(jnp.int32, (128, tok), 0) + r * 128
        col = lax.broadcasted_iota(jnp.int32, (128, tok), 1)
        same = jnp.concatenate([marks] * (tok // 128), axis=1) == key_seg
        bias_ref[r * 128 : (r + 1) * 128, :] = jnp.where(same & (col <= row), 0.0, NEG)
    for c in range(tok // CHUNK):
        t0 = c * CHUNK
        width = min(tok, -(-(t0 + CHUNK) // 128) * 128)
        bias = bias_ref[t0 : t0 + CHUNK, :width]
        for g in range(kv):
            scores = dot_t(queries_of(q_ref, t0, g, group), k_ref[g * tok : g * tok + width, :])
            scores = (scores.reshape(CHUNK, group, width) + bias[:, None, :]).reshape(CHUNK * group, width)
            top = jnp.max(scores, axis=1, keepdims=True)
            weights = jnp.exp2((scores - top) * scale).astype(jnp.bfloat16)
            rows = pl.ds(t0 * group, CHUNK * group)
            acc_ref[g, rows, :] = jnp.dot(
                weights, with_ones(v_ref[g * tok : g * tok + width, :]), preferred_element_type=jnp.float32
            )
            top_ref[g, rows, :] = jnp.broadcast_to(top, (CHUNK * group, 128))


def reach_of(k_ref, seg_ref, tok):
    marks = (seg_ref[...] + 1).astype(jnp.float32)
    first = marks[0:1, 0:1]
    usable = key_marks(k_ref, tok) == first
    reach = jnp.sum(jnp.where(marks == first, 1.0, 0.0)).astype(jnp.int32)
    any_key = jnp.max(jnp.where(usable, 1.0, 0.0)) > 0.5
    chunks = jnp.where(any_key, (reach + CHUNK - 1) // CHUNK, 0)
    return usable, reach, chunks


def next_tile(q_ref, k_ref, v_ref, seg_ref, acc_in, top_in, acc_ref, top_ref):
    tok, heads, hd = q_ref.shape
    kv = acc_ref.shape[0]
    group = heads // kv
    scale = hd**-0.5 * LOG2E
    usable, reach, chunks = reach_of(k_ref, seg_ref, tok)
    token = lax.broadcasted_iota(jnp.int32, (CHUNK * group, tok), 0) // group

    def body(c, _):
        t0 = pl.multiple_of(c * CHUNK, CHUNK)
        mask = usable & (token + t0 < reach)
        for g in range(kv):
            rows = pl.ds(pl.multiple_of(t0 * group, CHUNK * group), CHUNK * group)
            scores = dot_t(queries_of(q_ref, t0, g, group), k_ref[g * tok : (g + 1) * tok, :])
            scores = jnp.where(mask, scores, NEG)
            old = top_ref[g, rows, :]
            top = jnp.maximum(old, jnp.max(scores, axis=1, keepdims=True))
            weights = jnp.exp2((scores - top[:, :1]) * scale).astype(jnp.bfloat16)
            shrink = jnp.exp2((old - top) * scale)
            update = jnp.dot(
                weights, with_ones(v_ref[g * tok : (g + 1) * tok, :]), preferred_element_type=jnp.float32
            )
            acc_ref[g, rows, :] = acc_ref[g, rows, :] * jnp.concatenate([shrink, shrink], axis=1) + update
            top_ref[g, rows, :] = top
        return 0

    lax.fori_loop(0, chunks, body, 0)


def last_weights(q_ref, k_ref, seg_ref, acc_in, top_ref, acc_ref, w_ref):
    tok, heads, hd = q_ref.shape
    kv = acc_ref.shape[0]
    group = heads // kv
    scale = hd**-0.5 * LOG2E
    usable, reach, chunks = reach_of(k_ref, seg_ref, tok)
    token = lax.broadcasted_iota(jnp.int32, (CHUNK * group, tok), 0) // group

    def body(c, _):
        t0 = pl.multiple_of(c * CHUNK, CHUNK)
        mask = usable & (token + t0 < reach)
        for g in range(kv):
            rows = pl.ds(pl.multiple_of(t0 * group, CHUNK * group), CHUNK * group)
            scores = dot_t(queries_of(q_ref, t0, g, group), k_ref[g * tok : (g + 1) * tok, :])
            scores = jnp.where(mask, scores, NEG)
            old = top_ref[g, rows, :]
            top = jnp.maximum(old, jnp.max(scores, axis=1, keepdims=True))
            w_ref[g, rows, :] = jnp.exp2((scores - top[:, :1]) * scale).astype(jnp.bfloat16)
            shrink = jnp.exp2((old - top) * scale)
            acc_ref[g, rows, :] = acc_ref[g, rows, :] * jnp.concatenate([shrink, shrink], axis=1)
        return 0

    lax.fori_loop(0, chunks, body, 0)


def last_values(k_ref, v_ref, seg_ref, w_ref, acc_ref, out_ref):
    tok, heads, hd = out_ref.shape
    kv = acc_ref.shape[0]
    group = heads // kv
    _, _, chunks = reach_of(k_ref, seg_ref, tok)

    def finish(t0, states):
        parts = [(s[:, :hd] / s[:, hd:]).reshape(CHUNK, group, hd) for s in states]
        out_ref[pl.ds(t0, CHUNK), :, :] = jnp.concatenate(parts, axis=1).astype(jnp.bfloat16)

    def with_last(c, _):
        t0 = pl.multiple_of(c * CHUNK, CHUNK)
        rows = pl.ds(pl.multiple_of(t0 * group, CHUNK * group), CHUNK * group)
        states = []
        for g in range(kv):
            update = jnp.dot(
                w_ref[g, rows, :], with_ones(v_ref[g * tok : (g + 1) * tok, :]), preferred_element_type=jnp.float32
            )
            states.append(acc_ref[g, rows, :] + update)
        finish(t0, states)
        return 0

    def without(c, _):
        t0 = pl.multiple_of(c * CHUNK, CHUNK)
        rows = pl.ds(pl.multiple_of(t0 * group, CHUNK * group), CHUNK * group)
        finish(t0, [acc_ref[g, rows, :] for g in range(kv)])
        return 0

    lax.fori_loop(0, chunks, with_last, 0)
    lax.fori_loop(chunks, tok // CHUNK, without, 0)


def kernel(body, outs, ins, aliases=None, scratch=()):
    return pl.pallas_call(
        body,
        out_shape=outs,
        in_specs=[VMEM] * ins,
        out_specs=jax.tree.map(lambda _: VMEM, outs),
        input_output_aliases=aliases or {},
        scratch_shapes=scratch,
        compiler_params=pltpu.CompilerParams(vmem_limit_bytes=LIMIT),
    )


def local(queries, keys, values, seg_ids):
    tok, heads, hd = queries.shape
    kv = keys.shape[1]
    group = heads // kv
    bf16, f32 = jnp.bfloat16, jnp.float32
    seg_rows = seg_ids.reshape(tok // 128, 128)
    acc_shape = jax.ShapeDtypeStruct((kv, tok * group, 2 * hd), f32)
    top_shape = jax.ShapeDtypeStruct((kv, tok * group, 128), f32)

    def hop(x):
        return passed_along(x, 1)

    k0 = kernel(pack_keys, jax.ShapeDtypeStruct((kv * tok + 8, hd), bf16), 2)(keys, seg_rows)
    v0 = kernel(pack_values, jax.ShapeDtypeStruct((kv * tok, hd), bf16), 1)(values)
    k1, v1 = hop(k0), hop(v0)
    k2, v2 = hop(k1), hop(v1)
    k3, v3 = hop(k2), hop(v2)
    acc, top = kernel(own_tile, (acc_shape, top_shape), 3, scratch=[pltpu.VMEM((tok, tok), f32)])(queries, k0, v0)
    for kd, vd in ((k1, v1), (k2, v2)):
        acc, top = kernel(next_tile, (acc_shape, top_shape), 6, {4: 0, 5: 1})(queries, kd, vd, seg_rows, acc, top)
    acc, weights = kernel(
        last_weights, (acc_shape, jax.ShapeDtypeStruct((kv, tok * group, tok), bf16)), 5, {3: 0}
    )(queries, k3, seg_rows, acc, top)
    return kernel(last_values, jax.ShapeDtypeStruct((tok, heads, hd), bf16), 5)(k3, v3, seg_rows, weights, acc)


def solution(mesh):
    placed = (
        P(AXES, "head", None),
        P(AXES, "head", None),
        P(AXES, "head", None),
        P(AXES),
    )
    return jax.shard_map(
        local,
        mesh=mesh,
        in_specs=placed,
        out_specs=P(AXES, "head", None),
        check_vma=False,
    )
```

time: 96.6 us -> 58.8 us (0.61)
  the two profiles are of different devices: /device:TPU:24 before, /device:TPU:16 now
where the time goes in v1:
time: 58.8 us; the launch traced here: 58.5 us
  waiting for transfers between devices  21.4 us (36%)
  Pallas kernels  17.4 us (30%)
  starting transfers between devices  15.3 us (26%)
  local copies, waits for them, and re-layouts  4.38 us (7%)
    ppermute x6, waiting for transfers between devices, passed_along(): return lax.ppermute(x, AXES, pairs)  21.4 us
    ppermute x6, starting transfers between devices, passed_along(): return lax.ppermute(x, AXES, pairs)  15.3 us
    pallas_call x2, Pallas kernels, local(): kernel(next_tile, (acc_shape, top_shape), 6, {4: 0, 5: 1})  13.1 us
    unnamed x10, local copies, waits for them, and re-layouts  4.38 us
    pallas_call x1, Pallas kernels, local(): kernel(own_tile, (acc_shape, top_shape), 3, scratch=[pltpu.VMEM((tok, tok...  1.98 us
    pallas_call x1, Pallas kernels, local(): kernel(last_values, jax.ShapeDtypeStruct((tok, heads, hd), bf16), 5)  1.54 us
  transfers between devices with their start and end apart: 6, of which 4 were waited for; matrix products, arithmetic and copies ran while one was open for 0% of the time, Pallas kernels for 27%

profile of v1, /device:TPU:16, one launch (start us, length us, event | category | flops | bytes accessed | tf_op | source)
XLA Modules:
  0.0 58.5 jit_solution(550799504601979149)
XLA Ops:
  0.0 0.0 copy-start.1
  0.0 0.9 %copy-done.1 = bf16[256,2,128]{2,1,0:T(2,128)(2,1)S(1)} copy-done((bf16[256,2,128]{2,1,0:T(2,128)(2,1)S(1)}, bf16[256,2,128]{2,1,0:T(2,128)(2,1)}, u32[]{:S(2)}) %copy-start.1) | copy-done | bytes 131096
  0.9 0.0 copy-start.3
  0.9 0.7 %copy-done.3 = s32[256]{0:T(256)S(1)} copy-done((s32[256]{0:T(256)S(1)}, s32[256]{0:T(256)}, u32[]{:S(2)}) %copy-start.3) | copy-done | bytes 1048
  1.6 0.2 shard_map.46.k_ref
  1.8 3.8 %collective-permute-start = (bf16[520,128]{1,0:T(8,128)(2,1)S(1)}, bf16[520,128]{1,0:T(8,128)(2,1)S(1)}, u32[]{:S(2)}, u32[]{:S(2)}) collective-permute-start(bf16[520,128]{1,0:T(8,128)(2,1)S(1)} %shard_map.46.k_ref), channel_id=1, source_target_pairs={{0,4},{4,8},{8,12},{12,16},{16,20},{20,24},{24,28},{28,32},{32,36}... | collective-permute-start | bytes 399368 | tf_op jit(solution)/shard_map/ppermute | solution.py:21
  5.7 0.0 copy-start.2
  5.7 0.9 %copy-done.2 = bf16[256,2,128]{2,1,0:T(2,128)(2,1)S(1)} copy-done((bf16[256,2,128]{2,1,0:T(2,128)(2,1)S(1)}, bf16[256,2,128]{2,1,0:T(2,128)(2,1)}, u32[]{:S(2)}) %copy-start.2) | copy-done | bytes 131096
  6.6 0.2 shard_map.47.v_ref
  6.8 3.8 %collective-permute-start.3 = (bf16[512,128]{1,0:T(8,128)(2,1)S(1)}, bf16[512,128]{1,0:T(8,128)(2,1)S(1)}, u32[]{:S(2)}, u32[]{:S(2)}) collective-permute-start(bf16[512,128]{1,0:T(8,128)(2,1)S(1)} %shard_map.47.v_ref), channel_id=1, source_target_pairs={{0,4},{4,8},{8,12},{12,16},{16,20},{20,24},{24,28},{28,32},{32,36}... | collective-permute-start | bytes 393224 | tf_op jit(solution)/shard_map/ppermute | solution.py:21
  10.6 14.2 %collective-permute-done.k_ref = bf16[520,128]{1,0:T(8,128)(2,1)S(1)} collective-permute-done((bf16[520,128]{1,0:T(8,128)(2,1)S(1)}, bf16[520,128]{1,0:T(8,128)(2,1)S(1)}, u32[]{:S(2)}, u32[]{:S(2)}) %collective-permute-start) | collective-permute-done | bytes 133152 | tf_op jit(solution)/shard_map/ppermute | solution.py:21
  24.9 1.9 %collective-permute-start.1 = (bf16[520,128]{1,0:T(8,128)(2,1)S(1)}, bf16[520,128]{1,0:T(8,128)(2,1)S(1)}, u32[]{:S(2)}, u32[]{:S(2)}) collective-permute-start(bf16[520,128]{1,0:T(8,128)(2,1)S(1)} %collective-permute-done.k_ref), channel_id=1, source_target_pairs={{0,4},{4,8},{8,12},{12,16},{16,20},{20,24},{24,28},{28,32},{32,36}... | collective-permute-start | bytes 399368 | tf_op jit(solution)/shard_map/ppermute | solution.py:21
  26.8 1.1 %collective-permute-done.3.v_ref = bf16[512,128]{1,0:T(8,128)(2,1)S(1)} collective-permute-done((bf16[512,128]{1,0:T(8,128)(2,1)S(1)}, bf16[512,128]{1,0:T(8,128)(2,1)S(1)}, u32[]{:S(2)}, u32[]{:S(2)}) %collective-permute-start.3) | collective-permute-done | bytes 131104 | tf_op jit(solution)/shard_map/ppermute | solution.py:21
  27.9 1.9 %collective-permute-start.4 = (bf16[512,128]{1,0:T(8,128)(2,1)S(1)}, bf16[512,128]{1,0:T(8,128)(2,1)S(1)}, u32[]{:S(2)}, u32[]{:S(2)}) collective-permute-start(bf16[512,128]{1,0:T(8,128)(2,1)S(1)} %collective-permute-done.3.v_ref), channel_id=1, source_target_pairs={{0,4},{4,8},{8,12},{12,16},{16,20},{20,24},{24,28},{28,32},{32,36}... | collective-permute-start | bytes 393224 | tf_op jit(solution)/shard_map/ppermute | solution.py:21
  29.8 5.0 %collective-permute-done.1.k_ref = bf16[520,128]{1,0:T(8,128)(2,1)S(1)} collective-permute-done((bf16[520,128]{1,0:T(8,128)(2,1)S(1)}, bf16[520,128]{1,0:T(8,128)(2,1)S(1)}, u32[]{:S(2)}, u32[]{:S(2)}) %collective-permute-start.1) | collective-permute-done | bytes 133152 | tf_op jit(solution)/shard_map/ppermute | solution.py:21
  34.8 1.9 %collective-permute-start.2 = (bf16[520,128]{1,0:T(8,128)(2,1)S(1)}, bf16[520,128]{1,0:T(8,128)(2,1)S(1)}, u32[]{:S(2)}, u32[]{:S(2)}) collective-permute-start(bf16[520,128]{1,0:T(8,128)(2,1)S(1)} %collective-permute-done.1.k_ref), channel_id=1, source_target_pairs={{0,4},{4,8},{8,12},{12,16},{16,20},{20,24},{24,28},{28,32},{32,36}... | collective-permute-start | bytes 399368 | tf_op jit(solution)/shard_map/ppermute | solution.py:21
  36.8 1.0 %collective-permute-done.4.v_ref = bf16[512,128]{1,0:T(8,128)(2,1)S(1)} collective-permute-done((bf16[512,128]{1,0:T(8,128)(2,1)S(1)}, bf16[512,128]{1,0:T(8,128)(2,1)S(1)}, u32[]{:S(2)}, u32[]{:S(2)}) %collective-permute-start.4) | collective-permute-done | bytes 131104 | tf_op jit(solution)/shard_map/ppermute | solution.py:21
  37.8 1.9 %collective-permute-start.5 = (bf16[512,128]{1,0:T(8,128)(2,1)S(1)}, bf16[512,128]{1,0:T(8,128)(2,1)S(1)}, u32[]{:S(2)}, u32[]{:S(2)}) collective-permute-start(bf16[512,128]{1,0:T(8,128)(2,1)S(1)} %collective-permute-done.4.v_ref), channel_id=1, source_target_pairs={{0,4},{4,8},{8,12},{12,16},{16,20},{20,24},{24,28},{28,32},{32,36}... | collective-permute-start | bytes 393224 | tf_op jit(solution)/shard_map/ppermute | solution.py:21
  39.7 0.0 copy-start
  39.7 1.2 %copy-done = bf16[256,16,128]{2,1,0:T(8,128)(2,1)S(1)} copy-done((bf16[256,16,128]{2,1,0:T(8,128)(2,1)S(1)}, bf16[256,16,128]{2,1,0:T(8,128)(2,1)}, u32[]{:S(2)}) %copy-start) | copy-done | bytes 1048600
  40.9 2.0 %shard_map.48 = (f32[2,2048,256]{2,1,0:T(8,128)S(1)}, f32[2,2048,128]{2,1,0:T(8,128)S(1)}) custom-call(bf16[256,16,128]{2,1,0:T(8,128)(2,1)S(1)} %copy-done, bf16[520,128]{1,0:T(8,128)(2,1)S(1)} %shard_map.46.k_ref, bf16[512,128]{1,0:T(8,128)(2,1)S(1)} %shard_map.47.v_ref), custom_call_target="tpu_custom_call" | custom-call | tf_op jit(solution)/shard_map/pallas_call | solution.py:216
  42.9 0.0 copy-start.4
  42.9 0.7 %copy-done.4 = s32[256]{0:T(256)S(1)} copy-done((s32[256]{0:T(256)S(1)}, s32[256]{0:T(256)}, u32[]{:S(2)}) %copy-start.4) | copy-done | bytes 1048
  43.6 6.6 %shard_map.49 = (f32[2,2048,256]{2,1,0:T(8,128)S(1)}, f32[2,2048,128]{2,1,0:T(8,128)S(1)}) custom-call(bf16[256,16,128]{2,1,0:T(8,128)(2,1)S(1)} %copy-done, bf16[520,128]{1,0:T(8,128)(2,1)S(1)} %collective-permute-done.k_ref, bf16[512,128]{1,0:T(8,128)(2,1)S(1)} %collective-permute-done.3.v_ref, ...), custom_call_target="tpu_custom_call", output_to_operand_aliasing={{0}: (4, {}), {1}: (5, {})} | custom-call | tf_op jit(solution)/shard_map/pallas_call | solution.py:218
  50.1 6.6 %shard_map.50 = (f32[2,2048,256]{2,1,0:T(8,128)S(1)}, f32[2,2048,128]{2,1,0:T(8,128)S(1)}) custom-call(bf16[256,16,128]{2,1,0:T(8,128)(2,1)S(1)} %copy-done, bf16[520,128]{1,0:T(8,128)(2,1)S(1)} %collective-permute-done.1.k_ref, bf16[512,128]{1,0:T(8,128)(2,1)S(1)} %collective-permute-done.4.v_ref, ...), custom_call_target="tpu_custom_call", output_to_operand_aliasing={{0}: (4, {}), {1}: (5, {})} | custom-call | tf_op jit(solution)/shard_map/pallas_call | solution.py:218
  56.7 0.0 collective-permute-done.2.k_ref
  56.7 0.2 shard_map.51
  56.9 0.0 collective-permute-done.5.v_ref
  56.9 1.5 %shard_map.52 = bf16[256,16,128]{2,1,0:T(8,128)(2,1)} custom-call(bf16[520,128]{1,0:T(8,128)(2,1)S(1)} %collective-permute-done.2.k_ref, bf16[512,128]{1,0:T(8,128)(2,1)S(1)} %collective-permute-done.5.v_ref, s32[2,128]{1,0:T(2,128)S(1)} %bitcast.5, bf16[2,2048,256]{2,1,0:T(8,128)(2,1)S(1)} %get-tuple-element.19.w_ref, ...), custom_call_target="tpu_custom_call" | custom-call | tf_op jit(solution)/shard_map/pallas_call | solution.py:222
Async XLA Ops:
  0.0 0.9 %copy-start.1 = (bf16[256,2,128]{2,1,0:T(2,128)(2,1)S(1)}, bf16[256,2,128]{2,1,0:T(2,128)(2,1)}, u32[]{:S(2)}) copy-start(bf16[256,2,128]{2,1,0:T(2,128)(2,1)} %k_ref.1) | copy-start | bytes 393220
  0.9 0.7 %copy-start.3 = (s32[256]{0:T(256)S(1)}, s32[256]{0:T(256)}, u32[]{:S(2)}) copy-start(s32[256]{0:T(256)} %param.7) | copy-start | bytes 3076
  1.8 23.0 %collective-permute-start = (bf16[520,128]{1,0:T(8,128)(2,1)S(1)}, bf16[520,128]{1,0:T(8,128)(2,1)S(1)}, u32[]{:S(2)}, u32[]{:S(2)}) collective-permute-start(bf16[520,128]{1,0:T(8,128)(2,1)S(1)} %shard_map.46.k_ref), channel_id=1, source_target_pairs={{0,4},{4,8},{8,12},{12,16},{16,20},{20,24},{24,28},{28,32},{32,36}... | collective-permute-start | bytes 399368 | tf_op jit(solution)/shard_map/ppermute | solution.py:21
  5.7 0.9 %copy-start.2 = (bf16[256,2,128]{2,1,0:T(2,128)(2,1)S(1)}, bf16[256,2,128]{2,1,0:T(2,128)(2,1)}, u32[]{:S(2)}) copy-start(bf16[256,2,128]{2,1,0:T(2,128)(2,1)} %v_ref.1) | copy-start | bytes 393220
  6.8 21.1 %collective-permute-start.3 = (bf16[512,128]{1,0:T(8,128)(2,1)S(1)}, bf16[512,128]{1,0:T(8,128)(2,1)S(1)}, u32[]{:S(2)}, u32[]{:S(2)}) collective-permute-start(bf16[512,128]{1,0:T(8,128)(2,1)S(1)} %shard_map.47.v_ref), channel_id=1, source_target_pairs={{0,4},{4,8},{8,12},{12,16},{16,20},{20,24},{24,28},{28,32},{32,36}... | collective-permute-start | bytes 393224 | tf_op jit(solution)/shard_map/ppermute | solution.py:21
  24.9 10.0 %collective-permute-start.1 = (bf16[520,128]{1,0:T(8,128)(2,1)S(1)}, bf16[520,128]{1,0:T(8,128)(2,1)S(1)}, u32[]{:S(2)}, u32[]{:S(2)}) collective-permute-start(bf16[520,128]{1,0:T(8,128)(2,1)S(1)} %collective-permute-done.k_ref), channel_id=1, source_target_pairs={{0,4},{4,8},{8,12},{12,16},{16,20},{20,24},{24,28},{28,32},{32,36}... | collective-permute-start | bytes 399368 | tf_op jit(solution)/shard_map/ppermute | solution.py:21
  27.9 9.9 %collective-permute-start.4 = (bf16[512,128]{1,0:T(8,128)(2,1)S(1)}, bf16[512,128]{1,0:T(8,128)(2,1)S(1)}, u32[]{:S(2)}, u32[]{:S(2)}) collective-permute-start(bf16[512,128]{1,0:T(8,128)(2,1)S(1)} %collective-permute-done.3.v_ref), channel_id=1, source_target_pairs={{0,4},{4,8},{8,12},{12,16},{16,20},{20,24},{24,28},{28,32},{32,36}... | collective-permute-start | bytes 393224 | tf_op jit(solution)/shard_map/ppermute | solution.py:21
  34.8 21.9 %collective-permute-start.2 = (bf16[520,128]{1,0:T(8,128)(2,1)S(1)}, bf16[520,128]{1,0:T(8,128)(2,1)S(1)}, u32[]{:S(2)}, u32[]{:S(2)}) collective-permute-start(bf16[520,128]{1,0:T(8,128)(2,1)S(1)} %collective-permute-done.1.k_ref), channel_id=1, source_target_pairs={{0,4},{4,8},{8,12},{12,16},{16,20},{20,24},{24,28},{28,32},{32,36}... | collective-permute-start | bytes 399368 | tf_op jit(solution)/shard_map/ppermute | solution.py:21
  37.8 19.2 %collective-permute-start.5 = (bf16[512,128]{1,0:T(8,128)(2,1)S(1)}, bf16[512,128]{1,0:T(8,128)(2,1)S(1)}, u32[]{:S(2)}, u32[]{:S(2)}) collective-permute-start(bf16[512,128]{1,0:T(8,128)(2,1)S(1)} %collective-permute-done.4.v_ref), channel_id=1, source_target_pairs={{0,4},{4,8},{8,12},{12,16},{16,20},{20,24},{24,28},{28,32},{32,36}... | collective-permute-start | bytes 393224 | tf_op jit(solution)/shard_map/ppermute | solution.py:21
  39.7 1.2 %copy-start = (bf16[256,16,128]{2,1,0:T(8,128)(2,1)S(1)}, bf16[256,16,128]{2,1,0:T(8,128)(2,1)}, u32[]{:S(2)}) copy-start(bf16[256,16,128]{2,1,0:T(8,128)(2,1)} %q_ref.7) | copy-start | bytes 3145732
  42.9 0.7 %copy-start.4 = (s32[256]{0:T(256)S(1)}, s32[256]{0:T(256)}, u32[]{:S(2)}) copy-start(s32[256]{0:T(256)} %param.7) | copy-start | bytes 3076

commit v2 on v1

v2 whole, which is shorter than its diff:
```python
import jax
import jax.numpy as jnp
from jax import lax
from jax.experimental import pallas as pl
from jax.experimental.pallas import tpu as pltpu
from jax.sharding import PartitionSpec as P


AXES = ("dcn", "ctx")
LOG2E = 1.4426950408889634
NEG = -1e30
CHUNK = 64
HALF = 128
LIMIT = 24 * 1024 * 1024

VMEM = pl.BlockSpec(memory_space=pltpu.VMEM)
HBM = pl.BlockSpec(memory_space=pltpu.HBM)


def passed_along(x, by):
    count = lax.axis_size(AXES)
    pairs = [(i, i + by) for i in range(count) if 0 <= i + by < count]
    return lax.ppermute(x, AXES, pairs)


def prepare(k_hbm, v_hbm, seg_hbm, key_ref, val_ref, k_ref, v_ref, seg_ref, sems):
    tok, kv, _ = k_ref.shape
    rows = seg_ref.shape[0]
    copies = [
        pltpu.make_async_copy(src, dst, sems.at[n])
        for n, (src, dst) in enumerate(((k_hbm, k_ref), (seg_hbm, seg_ref), (v_hbm, v_ref)))
    ]
    for copy in copies:
        copy.start()

    def pack(src, dst):
        x = src[...].astype(jnp.float32)
        for g in range(kv):
            dst[g * tok : (g + 1) * tok, :] = x[:, g, :].astype(jnp.bfloat16)

    copies[0].wait()
    pack(k_ref, key_ref)
    copies[1].wait()
    marks = (seg_ref[...] + 1).astype(jnp.float32)
    pad = jnp.zeros((8 - rows, 128), jnp.float32)
    key_ref[kv * tok :, :] = jnp.concatenate([marks, pad], axis=0).astype(jnp.bfloat16)
    copies[2].wait()
    pack(v_ref, val_ref)


def wide(x, like):
    return jnp.concatenate([x] * (like.shape[1] // x.shape[1]), axis=1)


def dot_t(a, b):
    return lax.dot_general(a, b, (((1,), (1,)), ((), ())), preferred_element_type=jnp.float32)


def with_ones(vals):
    return jnp.concatenate([vals, jnp.ones(vals.shape, vals.dtype)], axis=1)


def marks_of(key_ref, tok):
    base = key_ref.shape[0] - 8
    tail = key_ref[base : base + 8, :].astype(jnp.float32)
    return jnp.concatenate([tail[r : r + 1, :] for r in range(tok // 128)], axis=1)


def own_tile(raw_ref, key_ref, val_ref, acc_ref, top_ref, q_ref, bias_ref):
    tok, heads, hd = raw_ref.shape
    kv = acc_ref.shape[0]
    group = heads // kv
    scale = hd**-0.5 * LOG2E
    key_seg = marks_of(key_ref, tok)
    for r in range(tok // 128):
        marks = jnp.broadcast_to(key_seg[:, r * 128 : (r + 1) * 128], (128, 128)).T
        row = lax.broadcasted_iota(jnp.int32, (128, tok), 0) + r * 128
        col = lax.broadcasted_iota(jnp.int32, (128, tok), 1)
        same = jnp.concatenate([marks] * (tok // 128), axis=1) == key_seg
        bias_ref[r * 128 : (r + 1) * 128, :] = jnp.where(same & (col <= row), 0.0, NEG)
    for c in range(tok // CHUNK):
        t0 = c * CHUNK
        width = min(tok, -(-(t0 + CHUNK) // 128) * 128)
        bias = bias_ref[t0 : t0 + CHUNK, :width]
        rows = slice(t0 * group, (t0 + CHUNK) * group)
        raw = raw_ref[t0 : t0 + CHUNK, :, :].astype(jnp.float32)
        for g in range(kv):
            q = raw[:, g * group : (g + 1) * group, :].reshape(CHUNK * group, hd).astype(jnp.bfloat16)
            q_ref[g, rows, :] = q
            scores = dot_t(q, key_ref[g * tok : g * tok + width, :])
            scores = (scores.reshape(CHUNK, group, width) + bias[:, None, :]).reshape(CHUNK * group, width)
            top = jnp.max(scores, axis=1, keepdims=True)
            weights = jnp.exp2((scores - top) * scale).astype(jnp.bfloat16)
            acc_ref[g, rows, :] = jnp.dot(
                weights, with_ones(val_ref[g * tok : g * tok + width, :]), preferred_element_type=jnp.float32
            )
            top_ref[g, rows, :] = jnp.broadcast_to(top, (CHUNK * group, 128))


def reach_of(own_ref, far_ref, tok):
    own = marks_of(own_ref, tok)
    first = own[:, 0:1]
    usable = marks_of(far_ref, tok) == first
    reach = jnp.sum(jnp.where(own == first, 1.0, 0.0)).astype(jnp.int32)
    found = jnp.sum(jnp.where(usable, 1.0, 0.0)).astype(jnp.int32)
    return usable, jnp.where(found > 0, reach, 0), found


def far_scores(q_ref, key_ref, g, rows, t0, reach, usable, lo, hi):
    tok = usable.shape[1]
    count = rows.stop - rows.start
    scores = dot_t(q_ref[g, rows, :], key_ref[g * tok + lo : g * tok + hi, :])
    group = count // CHUNK
    token = lax.broadcasted_iota(jnp.int32, (count, hi - lo), 0) // group + t0
    return jnp.where(usable[:, lo:hi] & (token < reach), scores, NEG)


def steps_of(group, h):
    for c in range(h * HALF // CHUNK, (h + 1) * HALF // CHUNK):
        yield c * CHUNK, slice(c * CHUNK * group, (c + 1) * CHUNK * group)


def next_tile(own_ref, q_ref, key_ref, val_ref, acc_in, top_in, acc_ref, top_ref):
    kv, count, hd = q_ref.shape
    tok = val_ref.shape[0] // kv
    group = count // tok
    scale = hd**-0.5 * LOG2E
    usable, reach, _ = reach_of(own_ref, key_ref, tok)
    for h in range(tok // HALF):

        @pl.when(reach > h * HALF)
        def _():
            for t0, rows in steps_of(group, h):
                for g in range(kv):
                    scores = far_scores(q_ref, key_ref, g, rows, t0, reach, usable, 0, tok)
                    old = top_ref[g, rows, :]
                    top = jnp.maximum(old, jnp.max(scores, axis=1, keepdims=True))
                    weights = jnp.exp2((scores - wide(top, scores)) * scale).astype(jnp.bfloat16)
                    shrink = jnp.exp2((old - top) * scale)
                    update = jnp.dot(
                        weights, with_ones(val_ref[g * tok : (g + 1) * tok, :]), preferred_element_type=jnp.float32
                    )
                    acc_ref[g, rows, :] = acc_ref[g, rows, :] * jnp.concatenate([shrink, shrink], axis=1) + update
                    top_ref[g, rows, :] = top


def last_weights(own_ref, q_ref, key_ref, acc_in, top_ref, acc_ref, w_ref):
    kv, count, hd = q_ref.shape
    tok = (key_ref.shape[0] - 8) // kv
    group = count // tok
    scale = hd**-0.5 * LOG2E
    usable, reach, _ = reach_of(own_ref, key_ref, tok)
    for h in range(tok // HALF):
        lo = h * HALF

        @pl.when(reach > lo)
        def _():
            for t0, rows in steps_of(group, h):
                for g in range(kv):
                    scores = far_scores(q_ref, key_ref, g, rows, t0, reach, usable, lo, tok)
                    old = top_ref[g, rows, :]
                    top = jnp.maximum(old, jnp.max(scores, axis=1, keepdims=True))
                    w_ref[g, rows, lo:] = jnp.exp2((scores - wide(top, scores)) * scale).astype(jnp.bfloat16)
                    shrink = jnp.exp2((old - top) * scale)
                    acc_ref[g, rows, :] = acc_ref[g, rows, :] * jnp.concatenate([shrink, shrink], axis=1)


def last_values(own_ref, key_ref, val_ref, w_ref, acc_ref, out_hbm, out_ref, sems):
    tok, heads, hd = out_ref.shape
    kv = acc_ref.shape[0]
    group = heads // kv
    _, reach, _ = reach_of(own_ref, key_ref, tok)
    copies = [
        pltpu.make_async_copy(
            out_ref.at[pl.ds(c * CHUNK, CHUNK)], out_hbm.at[pl.ds(c * CHUNK, CHUNK)], sems.at[c]
        )
        for c in range(tok // CHUNK)
    ]

    def finish(t0, states):
        parts = [(s[:, :hd] / s[:, hd:]).reshape(CHUNK, group, hd) for s in states]
        out_ref[t0 : t0 + CHUNK, :, :] = jnp.concatenate(parts, axis=1).astype(jnp.bfloat16)
        copies[t0 // CHUNK].start()

    for h in range(tok // HALF):
        lo = h * HALF

        @pl.when(reach > lo)
        def _():
            for t0, rows in steps_of(group, h):
                states = []
                for g in range(kv):
                    update = jnp.dot(
                        w_ref[g, rows, lo:],
                        with_ones(val_ref[g * tok + lo : (g + 1) * tok, :]),
                        preferred_element_type=jnp.float32,
                    )
                    states.append(acc_ref[g, rows, :] + update)
                finish(t0, states)

        @pl.when(reach <= lo)
        def _():
            for t0, rows in steps_of(group, h):
                finish(t0, [acc_ref[g, rows, :] for g in range(kv)])

    for copy in copies:
        copy.wait()


def kernel(body, outs, ins, aliases=None, scratch=(), out_specs=None):
    return pl.pallas_call(
        body,
        out_shape=outs,
        in_specs=ins,
        out_specs=out_specs or jax.tree.map(lambda _: VMEM, outs),
        input_output_aliases=aliases or {},
        scratch_shapes=scratch,
        compiler_params=pltpu.CompilerParams(vmem_limit_bytes=LIMIT),
    )


def local(queries, keys, values, seg_ids):
    tok, heads, hd = queries.shape
    kv = keys.shape[1]
    group = heads // kv
    bf16, f32 = jnp.bfloat16, jnp.float32
    struct = jax.ShapeDtypeStruct
    seg_rows = seg_ids.reshape(tok // 128, 128)
    state = (struct((kv, tok * group, 2 * hd), f32), struct((kv, tok * group, 128), f32))
    chunks = tok // CHUNK
    dma = pltpu.SemaphoreType.DMA

    def hop(x, by=1):
        return passed_along(x, by)

    k0, v0 = kernel(
        prepare,
        (struct((kv * tok + 8, hd), bf16), struct((kv * tok, hd), bf16)),
        [HBM] * 3,
        scratch=[
            pltpu.VMEM((tok, kv, hd), bf16),
            pltpu.VMEM((tok, kv, hd), bf16),
            pltpu.VMEM((tok // 128, 128), jnp.int32),
            dma((3,)),
        ],
    )(*(pltpu.with_memory_space_constraint(x, pltpu.HBM) for x in (keys, values, seg_rows)))
    k1, v1 = hop(k0), hop(v0)
    k2, v2 = hop(k1), hop(v1)
    k3, v3 = hop(k2), hop(v2)
    acc, top, q = kernel(
        own_tile,
        (*state, struct((kv, tok * group, hd), bf16)),
        [VMEM] * 3,
        scratch=[pltpu.VMEM((tok, tok), f32)],
    )(queries, k0, v0)
    for kd, vd in ((k1, v1), (k2, v2)):
        acc, top = kernel(next_tile, state, [VMEM] * 6, {4: 0, 5: 1})(k0, q, kd, vd, acc, top)
    acc, weights = kernel(
        last_weights, (state[0], struct((kv, tok * group, tok), bf16)), [VMEM] * 5, {3: 0}
    )(k0, q, k3, acc, top)
    return kernel(
        last_values,
        struct((tok, heads, hd), bf16),
        [VMEM] * 5,
        scratch=[pltpu.VMEM((tok, heads, hd), bf16), dma((chunks,))],
        out_specs=HBM,
    )(k0, k3, v3, weights, acc)


def solution(mesh):
    placed = (P(AXES, "head", None), P(AXES, "head", None), P(AXES, "head", None), P(AXES))
    return jax.shard_map(local, mesh=mesh, in_specs=placed, out_specs=P(AXES, "head", None), check_vma=False)
```

time: 58.8 us -> 50.7 us (0.86)
  the two profiles are of different devices: /device:TPU:16 before, /device:TPU:24 now
where the time goes in v2:
time: 50.7 us; the launch traced here: 50.4 us
  waiting for transfers between devices  25.4 us (50%)
  starting transfers between devices  15.3 us (30%)
  Pallas kernels  8.41 us (17%)
  local copies, waits for them, and re-layouts  1.22 us (2%)
    ppermute x6, waiting for transfers between devices, passed_along(): return lax.ppermute(x, AXES, pairs)  25.4 us
    ppermute x6, starting transfers between devices, passed_along(): return lax.ppermute(x, AXES, pairs)  15.3 us
    pallas_call x2, Pallas kernels, local(): kernel(next_tile, state, [VMEM] * 6, {4: 0, 5: 1})(k0, q, kd, vd, acc, top)  2.68 us
    pallas_call x1, Pallas kernels, local(): kernel(own_tile, (*state, struct((kv, tok * group, hd), bf16)), [VMEM] *...  1.78 us
    pallas_call x1, Pallas kernels, local(): kernel(last_values, struct((tok, heads, hd), bf16), [VMEM] * 5, scratch=[...  1.55 us
    pallas_call x1, Pallas kernels, local(): kernel(prepare, (struct((kv * tok + 8, hd), bf16), struct((kv * tok, hd),...  1.32 us
    unnamed x2, local copies, waits for them, and re-layouts  1.22 us
    pallas_call x1, Pallas kernels, local(): kernel(last_weights, (state[0], struct((kv, tok * group, tok), bf16)), [V...  1.09 us
  transfers between devices with their start and end apart: 6, of which 4 were waited for; matrix products, arithmetic and copies ran while one was open for 0% of the time, Pallas kernels for 11%

profile of v2, /device:TPU:24, one launch (start us, length us, event | category | flops | bytes accessed | tf_op | source)
XLA Modules:
  0.0 50.4 jit_solution(7439715468453472049)
XLA Ops:
  0.0 1.3 %shard_map.46 = (bf16[520,128]{1,0:T(8,128)(2,1)S(1)}, bf16[512,128]{1,0:T(8,128)(2,1)S(1)}) custom-call(bf16[256,2,128]{2,1,0:T(2,128)(2,1)} %k_hbm.1, bf16[256,2,128]{2,1,0:T(2,128)(2,1)} %v_hbm.1, s32[2,128]{1,0:T(2,128)} %bitcast.1), custom_call_target="tpu_custom_call" | custom-call | tf_op jit(solution)/shard_map/pallas_call | solution.py:236
  1.3 3.8 %collective-permute-start = (bf16[520,128]{1,0:T(8,128)(2,1)S(1)}, bf16[520,128]{1,0:T(8,128)(2,1)S(1)}, u32[]{:S(2)}, u32[]{:S(2)}) collective-permute-start(bf16[520,128]{1,0:T(8,128)(2,1)S(1)} %get-tuple-element.16.key_ref.own_ref), channel_id=1, source_target_pairs={{0,4},{4,8},{8,12},{12,16},{16,20},{20,24},{24,28},{28,32},{32,36}... | collective-permute-start | bytes 399368 | tf_op jit(solution)/shard_map/ppermute | solution.py:23
  5.2 3.8 %collective-permute-start.3 = (bf16[512,128]{1,0:T(8,128)(2,1)S(1)}, bf16[512,128]{1,0:T(8,128)(2,1)S(1)}, u32[]{:S(2)}, u32[]{:S(2)}) collective-permute-start(bf16[512,128]{1,0:T(8,128)(2,1)S(1)} %get-tuple-element.17.val_ref), channel_id=1, source_target_pairs={{0,4},{4,8},{8,12},{12,16},{16,20},{20,24},{24,28},{28,32},{32,36}... | collective-permute-start | bytes 393224 | tf_op jit(solution)/shard_map/ppermute | solution.py:23
  9.0 16.5 %collective-permute-done.key_ref = bf16[520,128]{1,0:T(8,128)(2,1)S(1)} collective-permute-done((bf16[520,128]{1,0:T(8,128)(2,1)S(1)}, bf16[520,128]{1,0:T(8,128)(2,1)S(1)}, u32[]{:S(2)}, u32[]{:S(2)}) %collective-permute-start) | collective-permute-done | bytes 133152 | tf_op jit(solution)/shard_map/ppermute | solution.py:23
  25.5 1.9 %collective-permute-start.1 = (bf16[520,128]{1,0:T(8,128)(2,1)S(1)}, bf16[520,128]{1,0:T(8,128)(2,1)S(1)}, u32[]{:S(2)}, u32[]{:S(2)}) collective-permute-start(bf16[520,128]{1,0:T(8,128)(2,1)S(1)} %collective-permute-done.key_ref), channel_id=1, source_target_pairs={{0,4},{4,8},{8,12},{12,16},{16,20},{20,24},{24,28},{28,32},{32,36}... | collective-permute-start | bytes 399368 | tf_op jit(solution)/shard_map/ppermute | solution.py:23
  27.4 0.0 collective-permute-done.3.val_ref
  27.5 1.9 %collective-permute-start.4 = (bf16[512,128]{1,0:T(8,128)(2,1)S(1)}, bf16[512,128]{1,0:T(8,128)(2,1)S(1)}, u32[]{:S(2)}, u32[]{:S(2)}) collective-permute-start(bf16[512,128]{1,0:T(8,128)(2,1)S(1)} %collective-permute-done.3.val_ref), channel_id=1, source_target_pairs={{0,4},{4,8},{8,12},{12,16},{16,20},{20,24},{24,28},{28,32},{32,36}... | collective-permute-start | bytes 393224 | tf_op jit(solution)/shard_map/ppermute | solution.py:23
  29.4 7.2 %collective-permute-done.1.key_ref = bf16[520,128]{1,0:T(8,128)(2,1)S(1)} collective-permute-done((bf16[520,128]{1,0:T(8,128)(2,1)S(1)}, bf16[520,128]{1,0:T(8,128)(2,1)S(1)}, u32[]{:S(2)}, u32[]{:S(2)}) %collective-permute-start.1) | collective-permute-done | bytes 133152 | tf_op jit(solution)/shard_map/ppermute | solution.py:23
  36.5 1.9 %collective-permute-start.2 = (bf16[520,128]{1,0:T(8,128)(2,1)S(1)}, bf16[520,128]{1,0:T(8,128)(2,1)S(1)}, u32[]{:S(2)}, u32[]{:S(2)}) collective-permute-start(bf16[520,128]{1,0:T(8,128)(2,1)S(1)} %collective-permute-done.1.key_ref), channel_id=1, source_target_pairs={{0,4},{4,8},{8,12},{12,16},{16,20},{20,24},{24,28},{28,32},{32,36}... | collective-permute-start | bytes 399368 | tf_op jit(solution)/shard_map/ppermute | solution.py:23
  38.5 0.0 collective-permute-done.4.val_ref
  38.5 1.9 %collective-permute-start.5 = (bf16[512,128]{1,0:T(8,128)(2,1)S(1)}, bf16[512,128]{1,0:T(8,128)(2,1)S(1)}, u32[]{:S(2)}, u32[]{:S(2)}) collective-permute-start(bf16[512,128]{1,0:T(8,128)(2,1)S(1)} %collective-permute-done.4.val_ref), channel_id=1, source_target_pairs={{0,4},{4,8},{8,12},{12,16},{16,20},{20,24},{24,28},{28,32},{32,36}... | collective-permute-start | bytes 393224 | tf_op jit(solution)/shard_map/ppermute | solution.py:23
  40.4 0.0 copy-start
  40.4 1.2 %copy-done = bf16[256,16,128]{2,1,0:T(8,128)(2,1)S(1)} copy-done((bf16[256,16,128]{2,1,0:T(8,128)(2,1)S(1)}, bf16[256,16,128]{2,1,0:T(8,128)(2,1)}, u32[]{:S(2)}) %copy-start) | copy-done | bytes 1048600
  41.6 1.8 %shard_map.47 = (f32[2,2048,256]{2,1,0:T(8,128)S(1)}, f32[2,2048,128]{2,1,0:T(8,128)S(1)}, bf16[2,2048,128]{2,1,0:T(8,128)(2,1)S(1)}) custom-call(bf16[256,16,128]{2,1,0:T(8,128)(2,1)S(1)} %copy-done, bf16[520,128]{1,0:T(8,128)(2,1)S(1)} %get-tuple-element.16.key_ref.own_ref, bf16[512,128]{1,0:T(8,128)(2,1)S(1)} %get-tuple-element.17.val_ref), custom_call_target="tpu_custom_call" | custom-call | tf_op jit(solution)/shard_map/pallas_call | solution.py:250
  43.4 1.3 %shard_map.48 = (f32[2,2048,256]{2,1,0:T(8,128)S(1)}, f32[2,2048,128]{2,1,0:T(8,128)S(1)}) custom-call(bf16[520,128]{1,0:T(8,128)(2,1)S(1)} %get-tuple-element.16.key_ref.own_ref, bf16[2,2048,128]{2,1,0:T(8,128)(2,1)S(1)} %get-tuple-element.18.q_ref, ...), custom_call_target="tpu_custom_call", output_to_operand_aliasing={{0}: (4, {}), {1}: (5, {})} | custom-call | tf_op jit(solution)/shard_map/pallas_call | solution.py:257
  44.8 1.3 %shard_map.49 = (f32[2,2048,256]{2,1,0:T(8,128)S(1)}, f32[2,2048,128]{2,1,0:T(8,128)S(1)}) custom-call(bf16[520,128]{1,0:T(8,128)(2,1)S(1)} %get-tuple-element.16.key_ref.own_ref, bf16[2,2048,128]{2,1,0:T(8,128)(2,1)S(1)} %get-tuple-element.18.q_ref, ...), custom_call_target="tpu_custom_call", output_to_operand_aliasing={{0}: (4, {}), {1}: (5, {})} | custom-call | tf_op jit(solution)/shard_map/pallas_call | solution.py:257
  46.1 1.3 %collective-permute-done.2.key_ref = bf16[520,128]{1,0:T(8,128)(2,1)S(1)} collective-permute-done((bf16[520,128]{1,0:T(8,128)(2,1)S(1)}, bf16[520,128]{1,0:T(8,128)(2,1)S(1)}, u32[]{:S(2)}, u32[]{:S(2)}) %collective-permute-start.2) | collective-permute-done | bytes 133152 | tf_op jit(solution)/shard_map/ppermute | solution.py:23
  47.4 1.1 %shard_map.50 = (f32[2,2048,256]{2,1,0:T(8,128)S(1)}, bf16[2,2048,256]{2,1,0:T(8,128)(2,1)S(1)}) custom-call(bf16[520,128]{1,0:T(8,128)(2,1)S(1)} %get-tuple-element.16.key_ref.own_ref, bf16[2,2048,128]{2,1,0:T(8,128)(2,1)S(1)} %get-tuple-element.18.q_ref, bf16[520,128]{1,0:T(8,128)(2,1)S(1)} %collective-permute-done.2.key_ref, ...), custom_call_target="tpu_custom_call", output_to_operand_aliasing={{0}: (3, {})} | custom-call | tf_op jit(solution)/shard_map/pallas_call | solution.py:258
  48.5 0.3 collective-permute-done.5.val_ref
  48.8 1.5 %shard_map.51 = bf16[256,16,128]{2,1,0:T(8,128)(2,1)} custom-call(bf16[520,128]{1,0:T(8,128)(2,1)S(1)} %get-tuple-element.16.key_ref.own_ref, bf16[520,128]{1,0:T(8,128)(2,1)S(1)} %collective-permute-done.2.key_ref, bf16[512,128]{1,0:T(8,128)(2,1)S(1)} %collective-permute-done.5.val_ref, bf16[2,2048,256]{2,1,0:T(8,128)(2,1)S(1)} %get-tuple-element.25.w_ref, ...), custom_call_target="tpu_custom_call" | custom-call | tf_op jit(solution)/shard_map/pallas_call | solution.py:261
Async XLA Ops:
  1.3 24.2 %collective-permute-start = (bf16[520,128]{1,0:T(8,128)(2,1)S(1)}, bf16[520,128]{1,0:T(8,128)(2,1)S(1)}, u32[]{:S(2)}, u32[]{:S(2)}) collective-permute-start(bf16[520,128]{1,0:T(8,128)(2,1)S(1)} %get-tuple-element.16.key_ref.own_ref), channel_id=1, source_target_pairs={{0,4},{4,8},{8,12},{12,16},{16,20},{20,24},{24,28},{28,32},{32,36}... | collective-permute-start | bytes 399368 | tf_op jit(solution)/shard_map/ppermute | solution.py:23
  5.2 22.3 %collective-permute-start.3 = (bf16[512,128]{1,0:T(8,128)(2,1)S(1)}, bf16[512,128]{1,0:T(8,128)(2,1)S(1)}, u32[]{:S(2)}, u32[]{:S(2)}) collective-permute-start(bf16[512,128]{1,0:T(8,128)(2,1)S(1)} %get-tuple-element.17.val_ref), channel_id=1, source_target_pairs={{0,4},{4,8},{8,12},{12,16},{16,20},{20,24},{24,28},{28,32},{32,36}... | collective-permute-start | bytes 393224 | tf_op jit(solution)/shard_map/ppermute | solution.py:23
  25.5 11.1 %collective-permute-start.1 = (bf16[520,128]{1,0:T(8,128)(2,1)S(1)}, bf16[520,128]{1,0:T(8,128)(2,1)S(1)}, u32[]{:S(2)}, u32[]{:S(2)}) collective-permute-start(bf16[520,128]{1,0:T(8,128)(2,1)S(1)} %collective-permute-done.key_ref), channel_id=1, source_target_pairs={{0,4},{4,8},{8,12},{12,16},{16,20},{20,24},{24,28},{28,32},{32,36}... | collective-permute-start | bytes 399368 | tf_op jit(solution)/shard_map/ppermute | solution.py:23
  27.5 11.0 %collective-permute-start.4 = (bf16[512,128]{1,0:T(8,128)(2,1)S(1)}, bf16[512,128]{1,0:T(8,128)(2,1)S(1)}, u32[]{:S(2)}, u32[]{:S(2)}) collective-permute-start(bf16[512,128]{1,0:T(8,128)(2,1)S(1)} %collective-permute-done.3.val_ref), channel_id=1, source_target_pairs={{0,4},{4,8},{8,12},{12,16},{16,20},{20,24},{24,28},{28,32},{32,36}... | collective-permute-start | bytes 393224 | tf_op jit(solution)/shard_map/ppermute | solution.py:23
  36.5 10.9 %collective-permute-start.2 = (bf16[520,128]{1,0:T(8,128)(2,1)S(1)}, bf16[520,128]{1,0:T(8,128)(2,1)S(1)}, u32[]{:S(2)}, u32[]{:S(2)}) collective-permute-start(bf16[520,128]{1,0:T(8,128)(2,1)S(1)} %collective-permute-done.1.key_ref), channel_id=1, source_target_pairs={{0,4},{4,8},{8,12},{12,16},{16,20},{20,24},{24,28},{28,32},{32,36}... | collective-permute-start | bytes 399368 | tf_op jit(solution)/shard_map/ppermute | solution.py:23
  38.5 10.4 %collective-permute-start.5 = (bf16[512,128]{1,0:T(8,128)(2,1)S(1)}, bf16[512,128]{1,0:T(8,128)(2,1)S(1)}, u32[]{:S(2)}, u32[]{:S(2)}) collective-permute-start(bf16[512,128]{1,0:T(8,128)(2,1)S(1)} %collective-permute-done.4.val_ref), channel_id=1, source_target_pairs={{0,4},{4,8},{8,12},{12,16},{16,20},{20,24},{24,28},{28,32},{32,36}... | collective-permute-start | bytes 393224 | tf_op jit(solution)/shard_map/ppermute | solution.py:23
  40.4 1.2 %copy-start = (bf16[256,16,128]{2,1,0:T(8,128)(2,1)S(1)}, bf16[256,16,128]{2,1,0:T(8,128)(2,1)}, u32[]{:S(2)}) copy-start(bf16[256,16,128]{2,1,0:T(8,128)(2,1)} %raw_ref.1) | copy-start | bytes 3145732

commit v3 on v2

--- a/solution.py
+++ b/solution.py
@@ -17,18 +17,25 @@
 HBM = pl.BlockSpec(memory_space=pltpu.HBM)
 
 
-def passed_along(x, by):
-    count = lax.axis_size(AXES)
-    pairs = [(i, i + by) for i in range(count) if 0 <= i + by < count]
+def passed_along(x, crossing=0):
+    count, inner = lax.axis_size(AXES), lax.axis_size("ctx")
+    if crossing:
+        pairs = [(i - crossing, i) for i in range(inner, count, inner)]
+    else:
+        pairs = [(i, i + 1) for i in range(count - 1) if (i + 1) % inner]
     return lax.ppermute(x, AXES, pairs)
 
 
-def prepare(k_hbm, v_hbm, seg_hbm, key_ref, val_ref, k_ref, v_ref, seg_ref, sems):
+def merge(a_ref, b_ref, out_ref):
+    out_ref[...] = (a_ref[...].astype(jnp.float32) + b_ref[...].astype(jnp.float32)).astype(out_ref.dtype)
+
+
+def prepare(k_hbm, v_hbm, seg_hbm, q_hbm, key_ref, val_ref, raw_ref, k_ref, v_ref, seg_ref, sems):
     tok, kv, _ = k_ref.shape
     rows = seg_ref.shape[0]
     copies = [
         pltpu.make_async_copy(src, dst, sems.at[n])
-        for n, (src, dst) in enumerate(((k_hbm, k_ref), (seg_hbm, seg_ref), (v_hbm, v_ref)))
+        for n, (src, dst) in enumerate(((k_hbm, k_ref), (seg_hbm, seg_ref), (v_hbm, v_ref), (q_hbm, raw_ref)))
     ]
     for copy in copies:
         copy.start()
@@ -46,6 +53,7 @@
     key_ref[kv * tok :, :] = jnp.concatenate([marks, pad], axis=0).astype(jnp.bfloat16)
     copies[2].wait()
     pack(v_ref, val_ref)
+    copies[3].wait()
 
 
 def wide(x, like):
@@ -144,13 +152,30 @@
                     top_ref[g, rows, :] = top
 
 
-def last_weights(own_ref, q_ref, key_ref, acc_in, top_ref, acc_ref, w_ref):
+def out_copies(buf_ref, out_hbm, sems):
+    return [
+        pltpu.make_async_copy(
+            buf_ref.at[pl.ds(c * CHUNK, CHUNK)], out_hbm.at[pl.ds(c * CHUNK, CHUNK)], sems.at[c]
+        )
+        for c in range(buf_ref.shape[0] // CHUNK)
+    ]
+
+
+def finish(buf_ref, t0, states):
+    hd = buf_ref.shape[-1]
+    parts = [(s[:, :hd] / s[:, hd:]).reshape(CHUNK, s.shape[0] // CHUNK, hd) for s in states]
+    buf_ref[t0 : t0 + CHUNK, :, :] = jnp.concatenate(parts, axis=1).astype(jnp.bfloat16)
+
+
+def last_weights(own_ref, q_ref, key_ref, acc_in, top_ref, acc_ref, w_ref, out_hbm, buf_ref, sems):
     kv, count, hd = q_ref.shape
     tok = (key_ref.shape[0] - 8) // kv
     group = count // tok
     scale = hd**-0.5 * LOG2E
     usable, reach, _ = reach_of(own_ref, key_ref, tok)
-    for h in range(tok // HALF):
+    copies = out_copies(buf_ref, out_hbm, sems)
+    halves = tok // HALF
+    for h in range(halves):
         lo = h * HALF
 
         @pl.when(reach > lo)
@@ -164,47 +189,44 @@
                     shrink = jnp.exp2((old - top) * scale)
                     acc_ref[g, rows, :] = acc_ref[g, rows, :] * jnp.concatenate([shrink, shrink], axis=1)
 
-
-def last_values(own_ref, key_ref, val_ref, w_ref, acc_ref, out_hbm, out_ref, sems):
-    tok, heads, hd = out_ref.shape
+    for h in range(halves):
+
+        @pl.when((reach <= h * HALF) & (reach > (h - 1) * HALF))
+        def _():
+            for part in range(h, halves):
+                for t0, rows in steps_of(group, part):
+                    finish(buf_ref, t0, [acc_ref[g, rows, :] for g in range(kv)])
+                    copies[t0 // CHUNK].start()
+            for c in range(h * HALF // CHUNK, len(copies)):
+                copies[c].wait()
+
+
+def last_values(own_ref, key_ref, val_ref, w_ref, acc_ref, out_in, out_hbm, buf_ref, sems):
+    tok, heads, _ = buf_ref.shape
     kv = acc_ref.shape[0]
     group = heads // kv
     _, reach, _ = reach_of(own_ref, key_ref, tok)
-    copies = [
-        pltpu.make_async_copy(
-            out_ref.at[pl.ds(c * CHUNK, CHUNK)], out_hbm.at[pl.ds(c * CHUNK, CHUNK)], sems.at[c]
-        )
-        for c in range(tok // CHUNK)
-    ]
-
-    def finish(t0, states):
-        parts = [(s[:, :hd] / s[:, hd:]).reshape(CHUNK, group, hd) for s in states]
-        out_ref[t0 : t0 + CHUNK, :, :] = jnp.concatenate(parts, axis=1).astype(jnp.bfloat16)
-        copies[t0 // CHUNK].start()
-
-    for h in range(tok // HALF):
-        lo = h * HALF
-
-        @pl.when(reach > lo)
+    copies = out_copies(buf_ref, out_hbm, sems)
+    halves = tok // HALF
+    for top in range(1, halves + 1):
+
+        @pl.when((reach > (top - 1) * HALF) & (reach <= top * HALF))
         def _():
-            for t0, rows in steps_of(group, h):
-                states = []
-                for g in range(kv):
-                    update = jnp.dot(
-                        w_ref[g, rows, lo:],
-                        with_ones(val_ref[g * tok + lo : (g + 1) * tok, :]),
-                        preferred_element_type=jnp.float32,
-                    )
-                    states.append(acc_ref[g, rows, :] + update)
-                finish(t0, states)
-
-        @pl.when(reach <= lo)
-        def _():
-            for t0, rows in steps_of(group, h):
-                finish(t0, [acc_ref[g, rows, :] for g in range(kv)])
-
-    for copy in copies:
-        copy.wait()
+            for h in range(top):
+                lo = h * HALF
+                for t0, rows in steps_of(group, h):
+                    states = []
+                    for g in range(kv):
+                        update = jnp.dot(
+                            w_ref[g, rows, lo:],
+                            with_ones(val_ref[g * tok + lo : (g + 1) * tok, :]),
+                            preferred_element_type=jnp.float32,
+                        )
+                        states.append(acc_ref[g, rows, :] + update)
+                    finish(buf_ref, t0, states)
+                    copies[t0 // CHUNK].start()
+            for c in range(top * HALF // CHUNK):
+                copies[c].wait()
 
 
 def kernel(body, outs, ins, aliases=None, scratch=(), out_specs=None):
@@ -230,41 +252,51 @@
     chunks = tok // CHUNK
     dma = pltpu.SemaphoreType.DMA
 
-    def hop(x, by=1):
-        return passed_along(x, by)
-
-    k0, v0 = kernel(
+    def hop(x, crossing=0):
+        return passed_along(x, crossing)
+
+    def joined(a, b):
+        return kernel(merge, struct(a.shape, a.dtype), [VMEM] * 2)(a, b)
+
+    k0, v0, raw = kernel(
         prepare,
-        (struct((kv * tok + 8, hd), bf16), struct((kv * tok, hd), bf16)),
-        [HBM] * 3,
+        (struct((kv * tok + 8, hd), bf16), struct((kv * tok, hd), bf16), struct(queries.shape, bf16)),
+        [HBM] * 4,
         scratch=[
             pltpu.VMEM((tok, kv, hd), bf16),
             pltpu.VMEM((tok, kv, hd), bf16),
             pltpu.VMEM((tok // 128, 128), jnp.int32),
-            dma((3,)),
+            dma((4,)),
         ],
-    )(*(pltpu.with_memory_space_constraint(x, pltpu.HBM) for x in (keys, values, seg_rows)))
-    k1, v1 = hop(k0), hop(v0)
-    k2, v2 = hop(k1), hop(v1)
-    k3, v3 = hop(k2), hop(v2)
+    )(*(pltpu.with_memory_space_constraint(x, pltpu.HBM) for x in (keys, values, seg_rows, queries)))
+    ki1, kc1 = hop(k0), hop(k0, 1)
+    vi1, vc1 = hop(v0), hop(v0, 1)
+    kc2, vc2 = hop(ki1, 1), hop(vi1, 1)
+    kc3, vc3 = hop(k0, 3), hop(v0, 3)
+    k1, v1 = joined(ki1, kc1), joined(vi1, vc1)
+    k2, v2 = joined(hop(k1), kc2), joined(hop(v1), vc2)
+    k3, v3 = joined(hop(k2), kc3), joined(hop(v2), vc3)
     acc, top, q = kernel(
         own_tile,
         (*state, struct((kv, tok * group, hd), bf16)),
         [VMEM] * 3,
         scratch=[pltpu.VMEM((tok, tok), f32)],
-    )(queries, k0, v0)
+    )(raw, k0, v0)
     for kd, vd in ((k1, v1), (k2, v2)):
         acc, top = kernel(next_tile, state, [VMEM] * 6, {4: 0, 5: 1})(k0, q, kd, vd, acc, top)
-    acc, weights = kernel(
-        last_weights, (state[0], struct((kv, tok * group, tok), bf16)), [VMEM] * 5, {3: 0}
+    buffers = [pltpu.VMEM((tok, heads, hd), bf16), dma((chunks,))]
+    result = struct((tok, heads, hd), bf16)
+    acc, weights, out = kernel(
+        last_weights,
+        (state[0], struct((kv, tok * group, tok), bf16), result),
+        [VMEM] * 5,
+        {3: 0},
+        scratch=buffers,
+        out_specs=(VMEM, VMEM, HBM),
     )(k0, q, k3, acc, top)
-    return kernel(
-        last_values,
-        struct((tok, heads, hd), bf16),
-        [VMEM] * 5,
-        scratch=[pltpu.VMEM((tok, heads, hd), bf16), dma((chunks,))],
-        out_specs=HBM,
-    )(k0, k3, v3, weights, acc)
+    return kernel(last_values, result, [VMEM] * 5 + [HBM], {5: 0}, scratch=buffers, out_specs=HBM)(
+        k0, k3, v3, weights, acc, out
+    )
 
 
 def solution(mesh):

time: 50.7 us -> 52.9 us (1.043)
  starting transfers between devices: 15.3 us -> 19.4 us
  waiting for transfers between devices: 25.4 us -> 23.5 us
  local copies, waits for them, and re-layouts: 1.22 us -> 0 us
  Pallas kernels: 8.41 us -> 9.47 us
    ppermute x6 -> x12, starting transfers between devices: 15.3 us -> 19.4 us  [passed_along(): return lax.ppermute(x, AXES, pairs)]
    ppermute x6 -> x12, waiting for transfers between devices: 25.4 us -> 23.5 us  [passed_along(): return lax.ppermute(x, AXES, pairs)]
    unnamed x2 -> x0, local copies, waits for them, and re-layouts: 1.22 us -> none
    pallas_call x2 -> x8, Pallas kernels: 2.63 us -> 3.58 us  [the longest x1 1.99 us: local(): kernel(last_weights, (state[0], struct((kv, tok * group, tok), bf16), res...]
  transfers between devices with their start and end apart: 6 -> 12, of which waited for: 4 -> 3; matrix products, arithmetic and copies ran while one was open for 0% -> 0% of each run, Pallas kernels for 11% -> 9%
where the time goes in v3:
time: 52.9 us; the launch traced here: 52.5 us
  waiting for transfers between devices  23.5 us (44%)
  starting transfers between devices  19.4 us (37%)
  Pallas kernels  9.47 us (18%)
    ppermute x12, waiting for transfers between devices, passed_along(): return lax.ppermute(x, AXES, pairs)  23.5 us
    ppermute x12, starting transfers between devices, passed_along(): return lax.ppermute(x, AXES, pairs)  19.4 us
    pallas_call x2, Pallas kernels, local(): kernel(next_tile, state, [VMEM] * 6, {4: 0, 5: 1})(k0, q, kd, vd, acc, top)  2.68 us
    pallas_call x1, Pallas kernels, local(): kernel(last_weights, (state[0], struct((kv, tok * group, tok), bf16), res...  1.99 us
    pallas_call x1, Pallas kernels, local(): kernel(own_tile, (*state, struct((kv, tok * group, hd), bf16)), [VMEM] *...  1.8 us
    pallas_call x1, Pallas kernels, local(): kernel(prepare, (struct((kv * tok + 8, hd), bf16), struct((kv * tok, hd),...  1.42 us
    pallas_call x1, Pallas kernels, local(): kernel(last_values, result, [VMEM] * 5 + [HBM], {5: 0}, scratch=buffers,...  1.38 us
  transfers between devices with their start and end apart: 12, of which 3 were waited for; matrix products, arithmetic and copies ran while one was open for 0% of the time, Pallas kernels for 9%

profile of v3, /device:TPU:24, one launch (start us, length us, event | category | flops | bytes accessed | tf_op | source)
XLA Modules:
  0.0 52.5 jit_solution(5727329032866856704)
XLA Ops:
  0.0 1.4 %shard_map.46 = (bf16[520,128]{1,0:T(8,128)(2,1)S(1)}, bf16[512,128]{1,0:T(8,128)(2,1)S(1)}, bf16[256,16,128]{2,1,0:T(8,128)(2,1)S(1)}) custom-call(bf16[256,2,128]{2,1,0:T(2,128)(2,1)} %k_hbm.1, bf16[256,2,128]{2,1,0:T(2,128)(2,1)} %v_hbm.1, s32[2,128]{1,0:T(2,128)} %bitcast.1, bf16[256,16,128]{2,1,0:T(8,128)(2,1)} %q_hbm.1), custom_call_target="tpu_custom_call" | custom-call | tf_op jit(solution)/shard_map/pallas_call | solution.py:261
  1.4 1.3 %collective-permute-start.1 = (bf16[520,128]{1,0:T(8,128)(2,1)S(1)}, bf16[520,128]{1,0:T(8,128)(2,1)S(1)}, u32[]{:S(2)}, u32[]{:S(2)}) collective-permute-start(bf16[520,128]{1,0:T(8,128)(2,1)S(1)} %get-tuple-element.18.key_ref.own_ref), channel_id=1, source_target_pairs={{124,128},{252,256},{380,384},{508,512},{636,640},{764,768},{892,8... | collective-permute-start | bytes 399368 | tf_op jit(solution)/shard_map/ppermute | solution.py:26
  2.7 3.2 %collective-permute-start = (bf16[520,128]{1,0:T(8,128)(2,1)S(1)}, bf16[520,128]{1,0:T(8,128)(2,1)S(1)}, u32[]{:S(2)}, u32[]{:S(2)}) collective-permute-start(bf16[520,128]{1,0:T(8,128)(2,1)S(1)} %get-tuple-element.18.key_ref.own_ref), channel_id=1, source_target_pairs={{0,4},{4,8},{8,12},{12,16},{16,20},{20,24},{24,28},{28,32},{32,36}... | collective-permute-start | bytes 399368 | tf_op jit(solution)/shard_map/ppermute | solution.py:26
  5.9 1.3 %collective-permute-start.7 = (bf16[512,128]{1,0:T(8,128)(2,1)S(1)}, bf16[512,128]{1,0:T(8,128)(2,1)S(1)}, u32[]{:S(2)}, u32[]{:S(2)}) collective-permute-start(bf16[512,128]{1,0:T(8,128)(2,1)S(1)} %get-tuple-element.19.val_ref), channel_id=1, source_target_pairs={{124,128},{252,256},{380,384},{508,512},{636,640},{764,768},{892,8... | collective-permute-start | bytes 393224 | tf_op jit(solution)/shard_map/ppermute | solution.py:26
  7.2 3.2 %collective-permute-start.6 = (bf16[512,128]{1,0:T(8,128)(2,1)S(1)}, bf16[512,128]{1,0:T(8,128)(2,1)S(1)}, u32[]{:S(2)}, u32[]{:S(2)}) collective-permute-start(bf16[512,128]{1,0:T(8,128)(2,1)S(1)} %get-tuple-element.19.val_ref), channel_id=1, source_target_pairs={{0,4},{4,8},{8,12},{12,16},{16,20},{20,24},{24,28},{28,32},{32,36}... | collective-permute-start | bytes 393224 | tf_op jit(solution)/shard_map/ppermute | solution.py:26
  10.4 13.9 %collective-permute-done.1.b_ref = bf16[520,128]{1,0:T(8,128)(2,1)S(1)} collective-permute-done((bf16[520,128]{1,0:T(8,128)(2,1)S(1)}, bf16[520,128]{1,0:T(8,128)(2,1)S(1)}, u32[]{:S(2)}, u32[]{:S(2)}) %collective-permute-start.1) | collective-permute-done | bytes 133152 | tf_op jit(solution)/shard_map/ppermute | solution.py:26
  24.4 0.0 collective-permute-done.a_ref
  24.4 1.3 %collective-permute-start.2 = (bf16[520,128]{1,0:T(8,128)(2,1)S(1)}, bf16[520,128]{1,0:T(8,128)(2,1)S(1)}, u32[]{:S(2)}, u32[]{:S(2)}) collective-permute-start(bf16[520,128]{1,0:T(8,128)(2,1)S(1)} %shard_map.47.key_ref), channel_id=1, source_target_pairs={{0,4},{4,8},{8,12},{12,16},{16,20},{20,24},{24,28},{28,32},{32,36}... | collective-permute-start | bytes 399368 | tf_op jit(solution)/shard_map/ppermute | solution.py:26
  25.7 1.3 %collective-permute-start.3 = (bf16[520,128]{1,0:T(8,128)(2,1)S(1)}, bf16[520,128]{1,0:T(8,128)(2,1)S(1)}, u32[]{:S(2)}, u32[]{:S(2)}) collective-permute-start(bf16[520,128]{1,0:T(8,128)(2,1)S(1)} %collective-permute-done.a_ref), channel_id=1, source_target_pairs={{124,128},{252,256},{380,384},{508,512},{636,640},{764,768},{892,8... | collective-permute-start | bytes 399368 | tf_op jit(solution)/shard_map/ppermute | solution.py:26
  27.0 0.0 collective-permute-done.7.b_ref
  27.0 0.0 collective-permute-done.6.a_ref
  27.1 1.3 %collective-permute-start.8 = (bf16[512,128]{1,0:T(8,128)(2,1)S(1)}, bf16[512,128]{1,0:T(8,128)(2,1)S(1)}, u32[]{:S(2)}, u32[]{:S(2)}) collective-permute-start(bf16[512,128]{1,0:T(8,128)(2,1)S(1)} %shard_map.50.val_ref), channel_id=1, source_target_pairs={{0,4},{4,8},{8,12},{12,16},{16,20},{20,24},{24,28},{28,32},{32,36}... | collective-permute-start | bytes 393224 | tf_op jit(solution)/shard_map/ppermute | solution.py:26
  28.4 1.3 %collective-permute-start.9 = (bf16[512,128]{1,0:T(8,128)(2,1)S(1)}, bf16[512,128]{1,0:T(8,128)(2,1)S(1)}, u32[]{:S(2)}, u32[]{:S(2)}) collective-permute-start(bf16[512,128]{1,0:T(8,128)(2,1)S(1)} %collective-permute-done.6.a_ref), channel_id=1, source_target_pairs={{124,128},{252,256},{380,384},{508,512},{636,640},{764,768},{892,8... | collective-permute-start | bytes 393224 | tf_op jit(solution)/shard_map/ppermute | solution.py:26
  29.7 1.3 %collective-permute-start.5 = (bf16[520,128]{1,0:T(8,128)(2,1)S(1)}, bf16[520,128]{1,0:T(8,128)(2,1)S(1)}, u32[]{:S(2)}, u32[]{:S(2)}) collective-permute-start(bf16[520,128]{1,0:T(8,128)(2,1)S(1)} %get-tuple-element.18.key_ref.own_ref), channel_id=1, source_target_pairs={{116,128},{244,256},{372,384},{500,512},{628,640},{756,768},{884,8... | collective-permute-start | bytes 399368 | tf_op jit(solution)/shard_map/ppermute | solution.py:26
  31.0 0.0 collective-permute-done.2.a_ref
  31.0 4.9 %collective-permute-done.3.b_ref = bf16[520,128]{1,0:T(8,128)(2,1)S(1)} collective-permute-done((bf16[520,128]{1,0:T(8,128)(2,1)S(1)}, bf16[520,128]{1,0:T(8,128)(2,1)S(1)}, u32[]{:S(2)}, u32[]{:S(2)}) %collective-permute-start.3) | collective-permute-done | bytes 133152 | tf_op jit(solution)/shard_map/ppermute | solution.py:26
  36.0 1.3 %collective-permute-start.4 = (bf16[520,128]{1,0:T(8,128)(2,1)S(1)}, bf16[520,128]{1,0:T(8,128)(2,1)S(1)}, u32[]{:S(2)}, u32[]{:S(2)}) collective-permute-start(bf16[520,128]{1,0:T(8,128)(2,1)S(1)} %shard_map.48.key_ref), channel_id=1, source_target_pairs={{0,4},{4,8},{8,12},{12,16},{16,20},{20,24},{24,28},{28,32},{32,36}... | collective-permute-start | bytes 399368 | tf_op jit(solution)/shard_map/ppermute | solution.py:26
  37.3 1.3 %collective-permute-start.11 = (bf16[512,128]{1,0:T(8,128)(2,1)S(1)}, bf16[512,128]{1,0:T(8,128)(2,1)S(1)}, u32[]{:S(2)}, u32[]{:S(2)}) collective-permute-start(bf16[512,128]{1,0:T(8,128)(2,1)S(1)} %get-tuple-element.19.val_ref), channel_id=1, source_target_pairs={{116,128},{244,256},{372,384},{500,512},{628,640},{756,768},{884,8... | collective-permute-start | bytes 393224 | tf_op jit(solution)/shard_map/ppermute | solution.py:26
  38.6 0.0 collective-permute-done.8.a_ref
  38.6 0.0 collective-permute-done.9.b_ref
  38.6 1.3 %collective-permute-start.10 = (bf16[512,128]{1,0:T(8,128)(2,1)S(1)}, bf16[512,128]{1,0:T(8,128)(2,1)S(1)}, u32[]{:S(2)}, u32[]{:S(2)}) collective-permute-start(bf16[512,128]{1,0:T(8,128)(2,1)S(1)} %shard_map.51.val_ref), channel_id=1, source_target_pairs={{0,4},{4,8},{8,12},{12,16},{16,20},{20,24},{24,28},{28,32},{32,36}... | collective-permute-start | bytes 393224 | tf_op jit(solution)/shard_map/ppermute | solution.py:26
  39.9 1.8 %shard_map.53 = (f32[2,2048,256]{2,1,0:T(8,128)S(1)}, f32[2,2048,128]{2,1,0:T(8,128)S(1)}, bf16[2,2048,128]{2,1,0:T(8,128)(2,1)S(1)}) custom-call(bf16[256,16,128]{2,1,0:T(8,128)(2,1)S(1)} %get-tuple-element.20.raw_ref, bf16[520,128]{1,0:T(8,128)(2,1)S(1)} %get-tuple-element.18.key_ref.own_ref, bf16[512,128]{1,0:T(8,128)(2,1)S(1)} %get-tuple-element.19.val_ref), custom_call_target="tpu_custom_call" | custom-call | tf_op jit(solution)/shard_map/pallas_call | solution.py:279
  41.7 1.3 %shard_map.54 = (f32[2,2048,256]{2,1,0:T(8,128)S(1)}, f32[2,2048,128]{2,1,0:T(8,128)S(1)}) custom-call(bf16[520,128]{1,0:T(8,128)(2,1)S(1)} %get-tuple-element.18.key_ref.own_ref, bf16[2,2048,128]{2,1,0:T(8,128)(2,1)S(1)} %get-tuple-element.21.q_ref, bf16[520,128]{1,0:T(8,128)(2,1)S(1)} %shard_map.47.key_ref, ...), custom_call_target="tpu_custom_call", output_to_operand_aliasing={{0}: (4, {}), {1}: (5, {})} | custom-call | tf_op jit(solution)/shard_map/pallas_call | solution.py:286
  43.1 1.3 %shard_map.55 = (f32[2,2048,256]{2,1,0:T(8,128)S(1)}, f32[2,2048,128]{2,1,0:T(8,128)S(1)}) custom-call(bf16[520,128]{1,0:T(8,128)(2,1)S(1)} %get-tuple-element.18.key_ref.own_ref, bf16[2,2048,128]{2,1,0:T(8,128)(2,1)S(1)} %get-tuple-element.21.q_ref, bf16[520,128]{1,0:T(8,128)(2,1)S(1)} %shard_map.48.key_ref, ...), custom_call_target="tpu_custom_call", output_to_operand_aliasing={{0}: (4, {}), {1}: (5, {})} | custom-call | tf_op jit(solution)/shard_map/pallas_call | solution.py:286
  44.4 4.6 %collective-permute-done.11.b_ref = bf16[512,128]{1,0:T(8,128)(2,1)S(1)} collective-permute-done((bf16[512,128]{1,0:T(8,128)(2,1)S(1)}, bf16[512,128]{1,0:T(8,128)(2,1)S(1)}, u32[]{:S(2)}, u32[]{:S(2)}) %collective-permute-start.11) | collective-permute-done | bytes 131104 | tf_op jit(solution)/shard_map/ppermute | solution.py:26
  49.0 0.0 collective-permute-done.10.a_ref
  49.1 0.0 collective-permute-done.5.b_ref
  49.1 0.0 collective-permute-done.4.a_ref
  49.1 2.0 %shard_map.56 = (f32[2,2048,256]{2,1,0:T(8,128)S(1)}, bf16[2,2048,256]{2,1,0:T(8,128)(2,1)S(1)}, bf16[256,16,128]{2,1,0:T(8,128)(2,1)}) custom-call(bf16[520,128]{1,0:T(8,128)(2,1)S(1)} %get-tuple-element.18.key_ref.own_ref, bf16[2,2048,128]{2,1,0:T(8,128)(2,1)S(1)} %get-tuple-element.21.q_ref, ...), custom_call_target="tpu_custom_call", output_to_operand_aliasing={{0}: (3, {})} | custom-call | tf_op jit(solution)/shard_map/pallas_call | solution.py:289
  51.2 1.4 %shard_map.57 = bf16[256,16,128]{2,1,0:T(8,128)(2,1)} custom-call(bf16[520,128]{1,0:T(8,128)(2,1)S(1)} %get-tuple-element.18.key_ref.own_ref, bf16[520,128]{1,0:T(8,128)(2,1)S(1)} %shard_map.49.key_ref, bf16[512,128]{1,0:T(8,128)(2,1)S(1)} %shard_map.52.val_ref, bf16[2,2048,256]{2,1,0:T(8,128)(2,1)S(1)} %get-tuple-element.28.w_ref, ...), custom_call_target="tpu_custom_call", output_to_operand_aliasing={{}: (5, {})} | custom-call | tf_op jit(solution)/shard_map/pallas_call | solution.py:297
  (6 shorter events, 0.2 us)
Async XLA Ops:
  1.4 22.9 %collective-permute-start.1 = (bf16[520,128]{1,0:T(8,128)(2,1)S(1)}, bf16[520,128]{1,0:T(8,128)(2,1)S(1)}, u32[]{:S(2)}, u32[]{:S(2)}) collective-permute-start(bf16[520,128]{1,0:T(8,128)(2,1)S(1)} %get-tuple-element.18.key_ref.own_ref), channel_id=1, source_target_pairs={{124,128},{252,256},{380,384},{508,512},{636,640},{764,768},{892,8... | collective-permute-start | bytes 399368 | tf_op jit(solution)/shard_map/ppermute | solution.py:26
  2.7 21.6 %collective-permute-start = (bf16[520,128]{1,0:T(8,128)(2,1)S(1)}, bf16[520,128]{1,0:T(8,128)(2,1)S(1)}, u32[]{:S(2)}, u32[]{:S(2)}) collective-permute-start(bf16[520,128]{1,0:T(8,128)(2,1)S(1)} %get-tuple-element.18.key_ref.own_ref), channel_id=1, source_target_pairs={{0,4},{4,8},{8,12},{12,16},{16,20},{20,24},{24,28},{28,32},{32,36}... | collective-permute-start | bytes 399368 | tf_op jit(solution)/shard_map/ppermute | solution.py:26
  5.9 21.1 %collective-permute-start.7 = (bf16[512,128]{1,0:T(8,128)(2,1)S(1)}, bf16[512,128]{1,0:T(8,128)(2,1)S(1)}, u32[]{:S(2)}, u32[]{:S(2)}) collective-permute-start(bf16[512,128]{1,0:T(8,128)(2,1)S(1)} %get-tuple-element.19.val_ref), channel_id=1, source_target_pairs={{124,128},{252,256},{380,384},{508,512},{636,640},{764,768},{892,8... | collective-permute-start | bytes 393224 | tf_op jit(solution)/shard_map/ppermute | solution.py:26
  7.2 19.8 %collective-permute-start.6 = (bf16[512,128]{1,0:T(8,128)(2,1)S(1)}, bf16[512,128]{1,0:T(8,128)(2,1)S(1)}, u32[]{:S(2)}, u32[]{:S(2)}) collective-permute-start(bf16[512,128]{1,0:T(8,128)(2,1)S(1)} %get-tuple-element.19.val_ref), channel_id=1, source_target_pairs={{0,4},{4,8},{8,12},{12,16},{16,20},{20,24},{24,28},{28,32},{32,36}... | collective-permute-start | bytes 393224 | tf_op jit(solution)/shard_map/ppermute | solution.py:26
  24.4 6.6 %collective-permute-start.2 = (bf16[520,128]{1,0:T(8,128)(2,1)S(1)}, bf16[520,128]{1,0:T(8,128)(2,1)S(1)}, u32[]{:S(2)}, u32[]{:S(2)}) collective-permute-start(bf16[520,128]{1,0:T(8,128)(2,1)S(1)} %shard_map.47.key_ref), channel_id=1, source_target_pairs={{0,4},{4,8},{8,12},{12,16},{16,20},{20,24},{24,28},{28,32},{32,36}... | collective-permute-start | bytes 399368 | tf_op jit(solution)/shard_map/ppermute | solution.py:26
  25.7 10.2 %collective-permute-start.3 = (bf16[520,128]{1,0:T(8,128)(2,1)S(1)}, bf16[520,128]{1,0:T(8,128)(2,1)S(1)}, u32[]{:S(2)}, u32[]{:S(2)}) collective-permute-start(bf16[520,128]{1,0:T(8,128)(2,1)S(1)} %collective-permute-done.a_ref), channel_id=1, source_target_pairs={{124,128},{252,256},{380,384},{508,512},{636,640},{764,768},{892,8... | collective-permute-start | bytes 399368 | tf_op jit(solution)/shard_map/ppermute | solution.py:26
  27.1 11.5 %collective-permute-start.8 = (bf16[512,128]{1,0:T(8,128)(2,1)S(1)}, bf16[512,128]{1,0:T(8,128)(2,1)S(1)}, u32[]{:S(2)}, u32[]{:S(2)}) collective-permute-start(bf16[512,128]{1,0:T(8,128)(2,1)S(1)} %shard_map.50.val_ref), channel_id=1, source_target_pairs={{0,4},{4,8},{8,12},{12,16},{16,20},{20,24},{24,28},{28,32},{32,36}... | collective-permute-start | bytes 393224 | tf_op jit(solution)/shard_map/ppermute | solution.py:26
  28.4 10.2 %collective-permute-start.9 = (bf16[512,128]{1,0:T(8,128)(2,1)S(1)}, bf16[512,128]{1,0:T(8,128)(2,1)S(1)}, u32[]{:S(2)}, u32[]{:S(2)}) collective-permute-start(bf16[512,128]{1,0:T(8,128)(2,1)S(1)} %collective-permute-done.6.a_ref), channel_id=1, source_target_pairs={{124,128},{252,256},{380,384},{508,512},{636,640},{764,768},{892,8... | collective-permute-start | bytes 393224 | tf_op jit(solution)/shard_map/ppermute | solution.py:26
  29.7 19.4 %collective-permute-start.5 = (bf16[520,128]{1,0:T(8,128)(2,1)S(1)}, bf16[520,128]{1,0:T(8,128)(2,1)S(1)}, u32[]{:S(2)}, u32[]{:S(2)}) collective-permute-start(bf16[520,128]{1,0:T(8,128)(2,1)S(1)} %get-tuple-element.18.key_ref.own_ref), channel_id=1, source_target_pairs={{116,128},{244,256},{372,384},{500,512},{628,640},{756,768},{884,8... | collective-permute-start | bytes 399368 | tf_op jit(solution)/shard_map/ppermute | solution.py:26
  36.0 13.1 %collective-permute-start.4 = (bf16[520,128]{1,0:T(8,128)(2,1)S(1)}, bf16[520,128]{1,0:T(8,128)(2,1)S(1)}, u32[]{:S(2)}, u32[]{:S(2)}) collective-permute-start(bf16[520,128]{1,0:T(8,128)(2,1)S(1)} %shard_map.48.key_ref), channel_id=1, source_target_pairs={{0,4},{4,8},{8,12},{12,16},{16,20},{20,24},{24,28},{28,32},{32,36}... | collective-permute-start | bytes 399368 | tf_op jit(solution)/shard_map/ppermute | solution.py:26
  37.3 11.8 %collective-permute-start.11 = (bf16[512,128]{1,0:T(8,128)(2,1)S(1)}, bf16[512,128]{1,0:T(8,128)(2,1)S(1)}, u32[]{:S(2)}, u32[]{:S(2)}) collective-permute-start(bf16[512,128]{1,0:T(8,128)(2,1)S(1)} %get-tuple-element.19.val_ref), channel_id=1, source_target_pairs={{116,128},{244,256},{372,384},{500,512},{628,640},{756,768},{884,8... | collective-permute-start | bytes 393224 | tf_op jit(solution)/shard_map/ppermute | solution.py:26
  38.6 10.4 %collective-permute-start.10 = (bf16[512,128]{1,0:T(8,128)(2,1)S(1)}, bf16[512,128]{1,0:T(8,128)(2,1)S(1)}, u32[]{:S(2)}, u32[]{:S(2)}) collective-permute-start(bf16[512,128]{1,0:T(8,128)(2,1)S(1)} %shard_map.51.val_ref), channel_id=1, source_target_pairs={{0,4},{4,8},{8,12},{12,16},{16,20},{20,24},{24,28},{28,32},{32,36}... | collective-permute-start | bytes 393224 | tf_op jit(solution)/shard_map/ppermute | solution.py:26
